TPU v7x, 32 devices: a whole 2x2x4 slice. The times are simulated.
32 devices in a mesh: ctx: 16 (over z, y, core), fsdp: 2 (over x).
Axes of the slice: x: 2, y: 2, z: 4, core: 2. Of those that a mesh axis runs over, the one named last changes fastest.
Arguments:
- tokens: bfloat16 [4096, 768], P(('fsdp', 'ctx')), may hold values from -6 to 6
- encoded: bfloat16 [4096, 768], P(('fsdp', 'ctx')), may hold values from -6 to 6
- cotangent: bfloat16 [4096, 768], P(('fsdp', 'ctx')), may hold values from -6 to 6
- tgt_lengths: int32 [2, 6], P('fsdp'), may hold values from 1 to 1984, 2048 in all within a row
- enc_lengths: int32 [2, 6], P('fsdp'), may hold values from 1 to 1984, 2048 in all within a row
- deal: int32 [2, 6], P('fsdp'), may hold values from 0 to 5, each once within a row
- ln_self: float32 [768], P('fsdp'), may hold values from 0.1 to 1.9
- ln_cross: float32 [768], P('fsdp'), may hold values from 0.1 to 1.9
- ln_ffn: float32 [768], P('fsdp'), may hold values from 0.1 to 1.9
- bias_table: float32 [32, 12], P('fsdp'), may hold values from -4 to 4
- self_query: float32 [768, 768], P('fsdp'), may hold values from -0.0546875 to 0.0546875
- self_key: float32 [768, 768], P('fsdp'), may hold values from -0.21875 to 0.21875
- self_value: float32 [768, 768], P('fsdp'), may hold values from -0.21875 to 0.21875
- self_output: float32 [768, 768], P('fsdp'), may hold values from -1.25 to 1.25
- cross_query: float32 [768, 768], P('fsdp'), may hold values from -0.0546875 to 0.0546875
- cross_key: float32 [768, 768], P('fsdp'), may hold values from -0.21875 to 0.21875
- cross_value: float32 [768, 768], P('fsdp'), may hold values from -0.21875 to 0.21875
- cross_output: float32 [768, 768], P('fsdp'), may hold values from -1.25 to 1.25
- ffn_inner: float32 [768, 3072], P('fsdp'), may hold values from -0.21875 to 0.21875
- ffn_outer: float32 [3072, 768], P('fsdp'), may hold values from -0.109375 to 0.109375
Outputs:
- output: float32 [4096, 768], P(('fsdp', 'ctx'))
- tokens_grad: float32 [4096, 768], P(('fsdp', 'ctx'))
- encoded_grad: float32 [4096, 768], P(('fsdp', 'ctx'))
- ln_self_grad: float32 [768], P('fsdp')
- ln_cross_grad: float32 [768], P('fsdp')
- ln_ffn_grad: float32 [768], P('fsdp')
- bias_table_grad: float32 [32, 12], P('fsdp')
- self_query_grad: float32 [768, 768], P('fsdp')
- self_key_grad: float32 [768, 768], P('fsdp')
- self_value_grad: float32 [768, 768], P('fsdp')
- self_output_grad: float32 [768, 768], P('fsdp')
- cross_query_grad: float32 [768, 768], P('fsdp')
- cross_key_grad: float32 [768, 768], P('fsdp')
- cross_value_grad: float32 [768, 768], P('fsdp')
- cross_output_grad: float32 [768, 768], P('fsdp')
- ffn_inner_grad: float32 [768, 3072], P('fsdp')
- ffn_outer_grad: float32 [3072, 768], P('fsdp')
Inputs may be any that keep to these rules, and one draw needn't show every extreme that they name: `tgt_lengths`: each row holds the lengths of the 6 target sequences of one group in packed order, summing to 2048; the longest is exactly 1984. `enc_lengths`: each row holds the lengths of the 6 encoder sequences of one group in packed order, summing to 2048; the longest is exactly 1984. `deal`: each row is a permutation of the 6 encoder sequences of the group.
All inputs are finite; a program needn't handle non-finite values.
Results may differ from a plain program's by a relative error of at most 0.03.
The roundings to bfloat16 on the way count: a program that leaves them out, or rounds other values in their place, can miss the bound.
Values may be sent and summed in bfloat16 or wider, within the bound.
No kernel may reach another device: no remote copies, remote signals or barrier semaphores. Data moves between devices by JAX's collectives and lax.ppermute only.
A program may use at most 192 MiB of HBM per device.

v0:
```python
import functools
import math

import jax
import jax.numpy as jnp
import numpy as np
from jax import lax
from jax.experimental import pallas as pl
from jax.experimental.pallas import tpu as pltpu
from jax.sharding import Mesh
from jax.sharding import PartitionSpec as P

HEADS = 12
HEAD_DIM = 64
BUCKETS = 32
EPS = 1e-06
NEG = -1e30
GELU_C = 0.7978845608028654
GELU_A = 0.044715

LOCAL = HEADS // 2
PAIRS = LOCAL // 2
HALF = LOCAL * HEAD_DIM
ROWS = 256
VMEM_LIMIT = 56 << 20

F32 = jnp.float32
BF16 = jnp.bfloat16


def bucket_edges():
    edges = []
    for level in range(1, 16):
        distance = 16
        while int(math.log(distance / 16.0) / math.log(8.0) * 16.0) < level:
            distance += 1
        edges.append(distance)
    return edges


def buckets_of(distances):
    clipped = np.maximum(np.asarray(distances), 0)
    large = np.full(clipped.shape, 16)
    for edge in bucket_edges():
        large = large + (clipped >= edge)
    return np.where(clipped < 16, clipped, large)


LANES = np.arange(2 * ROWS)
QK_DISTANCE = np.where(LANES <= ROWS, ROWS - LANES, 3 * ROWS - LANES)
KQ_DISTANCE = LANES
QK_ONEHOT = np.eye(BUCKETS, dtype=np.float32)[buckets_of(QK_DISTANCE)]
KQ_ONEHOT = np.eye(BUCKETS, dtype=np.float32)[buckets_of(KQ_DISTANCE)]


def dot_nt(left, right):
    return lax.dot_general(left, right, (((1,), (1,)), ((), ())), preferred_element_type=F32)


def dot_tn(left, right):
    return lax.dot_general(left, right, (((0,), (0,)), ((), ())), preferred_element_type=F32)


def dot_nn(left, right):
    return lax.dot_general(left, right, (((1,), (0,)), ((), ())), preferred_element_type=F32)


def spans(ref):
    starts, ends, at = [], [], jnp.int32(0)
    for i in range(ref.shape[1]):
        starts.append(at)
        at = at + ref[0, i]
        ends.append(at)
    return starts, ends


def seg_of(index, ends):
    found = jnp.zeros(index.shape, jnp.int32)
    for end in ends[:-1]:
        found = found + (index >= end).astype(jnp.int32)
    return found


def iota(shape, axis):
    return lax.broadcasted_iota(jnp.int32, shape, axis)


def split_pair(pair, sub=ROWS):
    low = iota((sub, pair.shape[1]), 1) < HEAD_DIM
    zero = jnp.zeros((sub, pair.shape[1]), pair.dtype)
    parts = []
    for at in range(0, pair.shape[0], sub):
        part = pair[at : at + sub]
        parts += [jnp.where(low, part, zero), jnp.where(low, zero, part)]
    return jnp.concatenate(parts, axis=0)


def head_rows(both, e, sub=ROWS):
    parts = [both[at + e * sub : at + (e + 1) * sub] for at in range(0, both.shape[0], 2 * sub)]
    return parts[0] if len(parts) == 1 else jnp.concatenate(parts, axis=0)


def join_pair(both, sub=ROWS):
    first = head_rows(both, 0, sub)
    return jnp.where(iota(first.shape, 1) < HEAD_DIM, first, head_rows(both, 1, sub))


def tiles_kernel(bias_ref, tiles_ref):
    def head(h, c):
        for which in range(2):
            row = bias_ref[pl.ds(8 * which + h, 1), :]
            rolled = pltpu.roll(jnp.broadcast_to(row, (ROWS, 2 * ROWS)), 0, 1, stride=1, stride_axis=0)
            first, second = (1, 2) if which == 0 else (2, 1)
            tiles_ref[which, first, h] = rolled[:, :ROWS].astype(BF16)
            tiles_ref[which, second, h] = rolled[:, ROWS:].astype(BF16)
            tiles_ref[which, 0, h] = jnp.broadcast_to(row[:, 2 * ROWS - 1 :], (ROWS, ROWS)).astype(BF16)
        return c

    lax.fori_loop(0, LOCAL, head, 0)


def lanes_of(p):
    return slice(p * 128, p * 128 + 128) if isinstance(p, int) else pl.ds(pl.multiple_of(p * 128, 128), 128)


def each_pair(body):
    for p in range(PAIRS):
        body(p)


def rms_inverse(value):
    return lax.rsqrt(jnp.mean(value * value, axis=-1, keepdims=True) + EPS)


def together(n):
    return PAIRS if n <= 2048 else 1


def attend(queries, keys, values, visit_scores, visit, sub, step, s_scr, mx_scr, l_scr, acc_scr, qs, o_ref, low_ref, lse_ref):
    count = s_scr.shape[0]
    lse_ref[...] = jnp.zeros_like(lse_ref)
    lane = iota((ROWS, 128), 1)

    def group(g):
        for c in range(count):
            qs[c] = split_pair(queries(g * count + c), sub)
        mx_scr[...] = jnp.full_like(mx_scr, NEG)

        def scores(j, rows, extra):
            at = pl.multiple_of(j * step, step)
            raws = [dot_nt(qs[c, rows], keys(g * count + c, at)) for c in range(count)]
            for c in range(count):
                value = extra(g * count + c, raws[c])
                s_scr[c, rows, pl.ds(at, step)] = value
                mx_scr[c, rows] = functools.reduce(
                    jnp.maximum, [value[:, i : i + 128] for i in range(0, step, 128)], mx_scr[c, rows]
                )

        visit_scores(scores)
        for c in range(count):
            mx_scr[c] = jnp.broadcast_to(jnp.max(mx_scr[c], axis=1, keepdims=True), mx_scr.shape[1:])
        l_scr[...] = jnp.zeros_like(l_scr)
        acc_scr[...] = jnp.zeros_like(acc_scr)

        def weigh(j, rows):
            at = pl.multiple_of(j * step, step)
            for c in range(count):
                weights = jnp.exp(s_scr[c, rows, pl.ds(at, step)] - mx_scr[c, rows, :1])
                l_scr[c, rows] += sum(weights[:, i : i + 128] for i in range(128, step, 128)) + weights[:, :128]
                acc_scr[c, rows] += dot_nn(weights.astype(BF16), values(g * count + c, at))

        visit(weigh)
        for c in range(count):
            p = g * count + c
            total = jnp.sum(l_scr[c], axis=1, keepdims=True)
            result = join_pair(acc_scr[c] / total, sub)
            o_ref[:, lanes_of(p)] = result
            low_ref[:, lanes_of(p)] = result.astype(BF16)
            both = mx_scr[c, :, :1] + jnp.log(total)
            lse = jnp.where(lane == 2 * p, head_rows(both, 0, sub), lse_ref[...])
            lse_ref[...] = jnp.where(lane == 2 * p + 1, head_rows(both, 1, sub), lse)

    if count == PAIRS:
        group(0)
    else:
        lax.fori_loop(0, PAIRS // count, lambda g, c: (group(g), c)[1], 0)


ATTEND = lambda n: [
    ((together(n), 2 * ROWS, n), F32), ((together(n), 2 * ROWS, 128), F32), ((together(n), 2 * ROWS, 128), F32),
    ((together(n), 2 * ROWS, 128), F32), ((together(n), 2 * ROWS, 128), BF16),
]


def set_rows(target, parts, side):
    if len(parts) == 1:
        target[...] = parts[0][...]
        return
    rows = parts[0].shape[0]
    target[pl.ds(pl.multiple_of(side * rows, rows), rows), :] = parts[0][...]
    target[pl.ds(pl.multiple_of((1 - side) * rows, rows), rows), :] = parts[1][...]


def first_of(base, ends):
    first = jnp.int32(0)
    for end in ends[:-1]:
        first = jnp.where(base >= end, end, first)
    return first


def self_stage_kernel(n_parts, at_ref, len_ref, xe_ref, gain_ref, tiles, *refs):
    parts, refs = refs[:n_parts], refs[n_parts:]
    qkv_ref, w_ref, o_ref, low_ref, lse_ref, s_scr, mx_scr, l_scr, acc_scr, qs = refs
    chip, side = at_ref[0], at_ref[2]
    set_rows(w_ref, parts, side)
    width = w_ref.shape[0]
    step = 512

    def body(i, c):
        at = pl.multiple_of(i * step, step)
        wide = xe_ref[pl.ds(at, step), :width].astype(F32)
        value = (wide * rms_inverse(wide) * gain_ref[...]).astype(BF16)
        result = dot_nn(value, w_ref[...])
        for j in range(qkv_ref.shape[0]):
            qkv_ref[j, pl.ds(at, step), :] = result[:, 128 * j : 128 * j + 128].astype(BF16)
        return c

    lax.fori_loop(0, xe_ref.shape[0] // step, body, 0)

    starts, ends = spans(len_ref)
    base = pl.multiple_of(chip * ROWS, ROWS)
    j_min = first_of(base, ends) // ROWS
    full_from = first_of(base + ROWS - 1, ends)
    q_row = base + iota((ROWS, 1), 0)
    q_seg = seg_of(q_row, ends)

    rows = slice(0, 2 * ROWS)

    def visit(block):
        lax.fori_loop(j_min, chip + 1, lambda j, c: (block(j, rows), c)[1], 0)

    def visit_scores(block):
        def body(j, c):
            at = pl.multiple_of(j * ROWS, ROWS)
            plain = (at >= full_from) & (j < chip - 1)

            def with_bias(bias):
                def extra(p, raw):
                    return jnp.concatenate([raw[:ROWS] + bias(2 * p), raw[ROWS:] + bias(2 * p + 1)], axis=0)

                block(j, rows, extra)

            @pl.when(plain)
            def _():
                with_bias(lambda h: tiles[0, 0, h, :1, :1].astype(F32))

            @pl.when(jnp.logical_not(plain))
            def _():
                k_row = at + iota((1, ROWS), 1)
                masked = jnp.where((q_seg == seg_of(k_row, ends)) & (k_row <= q_row), 0.0, NEG)
                tile = jnp.maximum(j - chip + 2, 0)
                with_bias(lambda h: tiles[0, tile, h].astype(F32) + masked)

            return c

        lax.fori_loop(j_min, chip + 1, body, 0)

    attend(
        lambda p: qkv_ref[p, pl.ds(base, ROWS), :],
        lambda p, at: qkv_ref[PAIRS + p, pl.ds(at, ROWS), :],
        lambda p, at: qkv_ref[2 * PAIRS + p, pl.ds(at, ROWS), :],
        visit_scores, visit, ROWS, ROWS, s_scr, mx_scr, l_scr, acc_scr, qs, o_ref, low_ref, lse_ref,
    )


def add_heads(low_ref, other_ref, w_ref, core):
    own = pl.ds(pl.multiple_of(core * HALF, HALF), HALF)
    other = pl.ds(pl.multiple_of((1 - core) * HALF, HALF), HALF)
    return dot_nn(low_ref[...], w_ref[own, :]) + dot_nn(other_ref[...], w_ref[other, :])


def cross_stage_kernel(n_parts, at_ref, len_ref, enc_ref, deal_ref, xe_ref, gain_ref, low_ref, other_ref, *refs):
    outs, mates, parts, refs = refs[:n_parts], refs[n_parts : 2 * n_parts], refs[2 * n_parts : 3 * n_parts], refs[3 * n_parts :]
    mid_ref, in_ref, q_ref, kv_ref, o_ref, low2_ref, lse_ref, so_ref, co_ref, wc_ref, refs = *refs[:10], refs[10:]
    s_scr, mx_scr, l_scr, acc_scr, qs = refs
    chip, core, side = at_ref[0], at_ref[1], at_ref[2]
    set_rows(wc_ref, parts, side)
    for pieces, column in ((outs, core), (mates, 1 - core)):
        lanes = pl.ds(pl.multiple_of(column * HALF, 128), HALF)
        for i, piece in enumerate(pieces):
            rows = piece.shape[0]
            at = pl.multiple_of((side if i == 0 else 1 - side) * rows, rows) if n_parts > 1 else 0
            so_ref[pl.ds(at, rows), lanes] = piece[:, :HALF]
            co_ref[pl.ds(at, rows), lanes] = piece[:, HALF:]
    width = so_ref.shape[0]
    base = pl.multiple_of(chip * ROWS, ROWS)
    mid = xe_ref[pl.ds(base, ROWS), :width].astype(F32) + add_heads(low_ref, other_ref, so_ref, core)
    mid_ref[...] = mid
    normed = (mid * rms_inverse(mid) * gain_ref[...]).astype(BF16)
    in_ref[...] = normed
    q_ref[...] = dot_nn(normed, wc_ref[:, :HALF]).astype(BF16)
    step = 512

    def body(i, c):
        at = pl.multiple_of(i * step, step)
        result = dot_nn(xe_ref[pl.ds(at, step), width:], wc_ref[:, HALF:])
        for j in range(kv_ref.shape[0]):
            kv_ref[j, pl.ds(at, step), :] = result[:, 128 * j : 128 * j + 128].astype(BF16)
        return c

    lax.fori_loop(0, xe_ref.shape[0] // step, body, 0)
    _, over, mask = cross_flags(chip, len_ref, enc_ref, deal_ref)
    blocks = kv_ref.shape[1] // KEYS

    def visit(block):
        over(blocks, lambda j, r: block(j, stacked(r)))

    def visit_scores(block):
        def body(j, r):
            masked = mask(j, r)
            block(j, stacked(r), lambda p, raw: raw + jnp.concatenate([masked, masked], axis=0))

        over(blocks, body)

    attend(
        lambda p: q_ref[:, lanes_of(p)],
        lambda p, at: kv_ref[p, pl.ds(at, KEYS), :],
        lambda p, at: kv_ref[PAIRS + p, pl.ds(at, KEYS), :],
        visit_scores, visit, SUB, KEYS, s_scr, mx_scr, l_scr, acc_scr, qs, o_ref, low2_ref, lse_ref,
    )


def gelu_parts(value):
    tangent = jnp.tanh(GELU_C * (value + GELU_A * value * value * value))
    result = 0.5 * value * (1.0 + tangent)
    slope = 0.5 * (1.0 + tangent) + 0.5 * value * (1.0 - tangent * tangent) * GELU_C * (
        1.0 + 3.0 * GELU_A * value * value
    )
    return (result, slope)


def own_rows(core, rows):
    return pl.ds(pl.multiple_of(core * rows, rows), rows)


def ffn_stage_kernel(n_parts, at_ref, mid_ref, gain_ref, low_ref, other_ref, co_ref, cot_ref, mate_ref, *refs):
    inner, outer, refs = refs[:n_parts], refs[n_parts : 2 * n_parts], refs[2 * n_parts :]
    late_ref, in_ref, hid_ref, dpre_ref, cot_out, keep_ref, send_ref, e_ref, wi_ref, wo_ref, part_scr = refs
    core, side = at_ref[1], at_ref[2]
    rows = cot_ref.shape[0]
    set_rows(wi_ref, inner, side)
    set_rows(wo_ref, outer, side)
    cot_out[own_rows(core, rows), :] = cot_ref[...]
    cot_out[own_rows(1 - core, rows), :] = mate_ref[...]
    late = mid_ref[...] + add_heads(low_ref, other_ref, co_ref, core)
    late_ref[...] = late
    normed = (late * rms_inverse(late) * gain_ref[...]).astype(BF16)
    in_ref[...] = normed
    columns = 512

    def body(i, c):
        at = pl.multiple_of(i * columns, columns)
        activated, slope = gelu_parts(dot_nn(normed, wi_ref[:, pl.ds(at, columns)]))
        hid_ref[:, pl.ds(at, columns)] = activated.astype(BF16)
        grads = dot_nt(cot_out[...], wo_ref[pl.ds(at, columns), :])
        dpre_ref[:, pl.ds(at, columns)] = (grads * slope).astype(BF16)
        return c

    lax.fori_loop(0, wi_ref.shape[1] // columns, body, 0)
    e_ref[...] = dot_nt(dpre_ref[...], wi_ref[...])
    part_scr[...] = dot_nn(hid_ref[...], wo_ref[...])
    keep_ref[...] = part_scr[own_rows(core, rows), :] + late_ref[own_rows(core, rows), :]
    send_ref[...] = part_scr[own_rows(1 - core, rows), :]


def ffn_grads_kernel(n_sides, at_ref, hid_ref, cot_ref, in_ref, dpre_ref, *outs):
    side = at_ref[2]
    rows = in_ref.shape[1] // n_sides
    width = cot_ref.shape[1]
    if n_sides != 2:
        outs[0][...] = dot_tn(hid_ref[...], cot_ref[...])
        outs[1][...] = dot_tn(in_ref[...], dpre_ref[...])
        return
    keep_ref, send_ref = outs
    for owner in range(2):
        for mine, target in ((True, keep_ref), (False, send_ref)):

            @pl.when((side == owner) == mine)
            def _():
                for part in range(2):
                    units = slice((2 * owner + part) * rows, (2 * owner + part + 1) * rows)
                    block = dot_tn(hid_ref[:, units], cot_ref[...])
                    target[:, part * width : (part + 1) * width] = block.astype(target.dtype)
                block = dot_tn(in_ref[:, owner * rows : (owner + 1) * rows], dpre_ref[...])
                target[:, 2 * width :] = block.astype(target.dtype)


def norm_grad(value, gain, grad):
    inverse = rms_inverse(value)
    scaled = grad * gain
    cubed = inverse * inverse * inverse
    dvalue = inverse * scaled - value * cubed * jnp.mean(scaled * value, axis=-1, keepdims=True)
    return dvalue, jnp.sum(grad * value * inverse, axis=0, keepdims=True)


KEYS = 2 * ROWS
SUB = ROWS


def cross_flags(chip, len_ref, enc_ref, deal_ref):
    starts, ends = spans(len_ref)
    e_starts, e_ends = spans(enc_ref)
    base = chip * ROWS
    ranges = []
    for i in range(len(ends)):
        low, high = jnp.int32(0), jnp.int32(0)
        for e in range(len(e_ends)):
            hit = deal_ref[0, i] == e
            low = jnp.where(hit, e_starts[e], low)
            high = jnp.where(hit, e_ends[e], high)
        ranges.append((starts[i], ends[i], low, high))

    def wanted(at, first, count):
        found = jnp.bool_(False)
        for start, end, low, high in ranges:
            live = (start < base + first + count) & (end > base + first)
            found = found | (live & (low < at + KEYS) & (high > at))
        return found

    def visit(blocks, body):
        def inner(j, c):
            for r in range(ROWS // SUB):

                @pl.when(wanted(j * KEYS, r * SUB, SUB))
                def _():
                    body(j, r)

            return c

        lax.fori_loop(0, blocks, inner, 0)

    q_seg = seg_of(base + iota((ROWS, 1), 0), ends)
    q_pair = jnp.zeros((ROWS, 1), jnp.int32)
    for i in range(len(ends)):
        q_pair = q_pair + jnp.where(q_seg == i, deal_ref[0, i], 0)

    def mask(j, r):
        k_seg = seg_of(j * KEYS + iota((1, KEYS), 1), e_ends)
        return jnp.where(q_pair[r * SUB : (r + 1) * SUB] == k_seg, 0.0, NEG)

    return wanted, visit, mask


def stacked(r):
    return slice(2 * r * SUB, 2 * (r + 1) * SUB)


def row_stats(go_ref, o_ref, lse_ref, gs, lse_scr, delta_scr, sub=ROWS):
    lane = iota((ROWS, 128), 1)
    low = lane < HEAD_DIM
    for p in range(PAIRS):
        grads = go_ref[:, lanes_of(p)]
        gs[p] = split_pair(grads, sub)
        product = grads.astype(F32) * o_ref[:, lanes_of(p)]
        for i in range(2):
            part = jnp.where(low if i == 0 else ~low, product, 0.0)
            delta = jnp.sum(part, axis=1, keepdims=True)
            lse = jnp.sum(jnp.where(lane == 2 * p + i, lse_ref[...], 0.0), axis=1, keepdims=True)
            for at in range(0, ROWS, sub):
                rows = slice(2 * at + i * sub, 2 * at + (i + 1) * sub)
                delta_scr[p, rows] = jnp.broadcast_to(delta[at : at + sub], (sub, 128))
                lse_scr[p, rows] = jnp.broadcast_to(lse[at : at + sub], (sub, 128))


def self_query_grad_kernel(
    at_ref, len_ref, tiles, qkv_ref, go_ref, o_ref, lse_ref, dq_ref, dist_ref,
    qs, gs, lse_scr, delta_scr, dq_scr, ds_scr, far_scr,
):
    chip = at_ref[0]
    starts, ends = spans(len_ref)
    base = pl.multiple_of(chip * ROWS, ROWS)
    first = first_of(base, ends)
    row_stats(go_ref, o_ref, lse_ref, gs, lse_scr, delta_scr)

    def start(p):
        qs[p] = split_pair(qkv_ref[p, pl.ds(base, ROWS), :])

    each_pair(start)
    dq_scr[...] = jnp.zeros_like(dq_scr)
    ds_scr[...] = jnp.zeros_like(ds_scr)
    far_scr[...] = jnp.zeros_like(far_scr)
    full_from = first_of(base + ROWS - 1, ends)
    q_row = base + iota((ROWS, 1), 0)
    q_seg = seg_of(q_row, ends)

    def block(j, _):
        at = pl.multiple_of(j * ROWS, ROWS)
        plain = (at >= full_from) & (j < chip - 1)

        def gradients(extra, near):
            raws = [dot_nt(qs[p], qkv_ref[PAIRS + p, pl.ds(at, ROWS), :]) for p in range(PAIRS)]
            dprobs = [dot_nt(gs[p], qkv_ref[2 * PAIRS + p, pl.ds(at, ROWS), :]) for p in range(PAIRS)]
            for p in range(PAIRS):
                grads = []
                for i in range(2):
                    h = 2 * p + i
                    rows = slice(i * ROWS, (i + 1) * ROWS)
                    probs = jnp.exp(extra(h, raws[p][rows]) - lse_scr[p, rows, :1])
                    ds = (probs * (dprobs[p][rows] - delta_scr[p, rows, :1])).astype(BF16)
                    if near is None:
                        far_scr[h] += jnp.sum(ds.astype(F32).reshape(ROWS // 8, 8, ROWS), axis=0)
                    else:
                        ds_scr[near, h] += ds.astype(F32)
                    grads.append(ds)
                dq_scr[p] += dot_nn(jnp.concatenate(grads, axis=0), qkv_ref[PAIRS + p, pl.ds(at, ROWS), :])

        @pl.when(plain)
        def _():
            gradients(lambda h, raw: raw + tiles[0, 0, h, :1, :1].astype(F32), None)

        @pl.when(jnp.logical_not(plain))
        def _():
            k_row = at + iota((1, ROWS), 1)
            masked = jnp.where((q_seg == seg_of(k_row, ends)) & (k_row <= q_row), 0.0, NEG)
            tile = jnp.maximum(j - chip + 2, 0)
            gradients(lambda h, raw: raw + (tiles[0, tile, h].astype(F32) + masked), tile)

        return 0

    lax.fori_loop(first // ROWS, chip + 1, block, 0)
    dist_ref[...] = jnp.zeros_like(dist_ref)
    lanes = iota((1, 2 * ROWS), 1)
    for p in range(PAIRS):
        dq_ref[:, 128 * p : 128 * p + 128] = join_pair(dq_scr[p]).astype(BF16)

    def fold(h, c):
        folded = jnp.concatenate([ds_scr[1, h], ds_scr[2, h]], axis=1)
        rows = ROWS
        while rows > 1:
            rows //= 2
            folded = folded[:rows] + pltpu.roll(folded[rows:], 2 * ROWS - rows, 1)
        far = jnp.sum(ds_scr[0, h], axis=0, keepdims=True) + jnp.sum(far_scr[h], axis=0, keepdims=True)
        far = jnp.sum(far, axis=1, keepdims=True)
        dist_ref[pl.ds(h, 1), :] = folded + jnp.where(lanes == 2 * ROWS - 1, far, 0.0)
        return c

    lax.fori_loop(0, LOCAL, fold, 0)


def self_key_stage_kernel(
    n_sides, at_ref, len_ref, tiles, qkv_ref, message_ref, so_ref, dq_ref, w_ref, x_ref, gain_ref, small_ref,
    keep_ref, send_ref, *refs,
):
    *outs, go_ref, stat_ref, ks, vs, dk_scr, dv_scr, dqkv_scr, h_scr, e_scr, grads_ref = refs
    chip, core = at_ref[0], at_ref[1]
    starts, ends = spans(len_ref)
    base = pl.multiple_of(chip * ROWS, ROWS)
    last = ends[-1]
    for end in reversed(ends[:-1]):
        last = jnp.where(base + ROWS - 1 < end, end, last)
    stop = (last - 1) // ROWS + 1
    full_to = ends[-1]
    for end in reversed(ends[:-1]):
        full_to = jnp.where(base < end, end, full_to)
    heads = own_rows(core, HALF)
    half = ROWS // 2

    def receive(i, c):
        both = [message_ref[2 * i + e, :half, :] for e in range(2)]
        result = dot_nt(jnp.concatenate(both, axis=0), so_ref[heads, :])
        for p in range(PAIRS):
            go_ref[p, pl.ds(pl.multiple_of(i * ROWS, ROWS), ROWS), :] = result[:, 128 * p : 128 * p + 128].astype(BF16)
        parts = message_ref[2 * i + core, half:, :].astype(F32)
        stat_ref[i] = parts[:, :ROWS] + parts[:, ROWS : 2 * ROWS] + parts[:, 2 * ROWS :]
        return c

    lax.fori_loop(chip, stop, receive, 0)

    def start(p):
        ks[p] = split_pair(qkv_ref[PAIRS + p, pl.ds(base, ROWS), :])
        vs[p] = split_pair(qkv_ref[2 * PAIRS + p, pl.ds(base, ROWS), :])

    each_pair(start)
    dk_scr[...] = jnp.zeros_like(dk_scr)
    dv_scr[...] = jnp.zeros_like(dv_scr)
    k_row = base + iota((ROWS, 1), 0)
    k_seg = seg_of(k_row, ends)

    def block(i, _):
        at = pl.multiple_of(i * ROWS, ROWS)
        plain = (at + ROWS <= full_to) & (i > chip + 1)

        def gradients(extra):
            raws = [dot_nt(ks[p], qkv_ref[p, pl.ds(at, ROWS), :]) for p in range(PAIRS)]
            dprobs = [dot_nt(vs[p], go_ref[p, pl.ds(at, ROWS), :]) for p in range(PAIRS)]
            for p in range(PAIRS):
                weights, dscores = [], []
                for e in range(2):
                    rows = slice(e * ROWS, (e + 1) * ROWS)
                    h = 2 * p + e
                    probs = jnp.exp(extra(h, raws[p][rows]) - stat_ref[i, h : h + 1, :])
                    weights.append(probs.astype(BF16))
                    dscores.append((probs * (dprobs[p][rows] - stat_ref[i, 8 + h : 9 + h, :])).astype(BF16))
                dv_scr[p] += dot_nn(jnp.concatenate(weights, axis=0), go_ref[p, pl.ds(at, ROWS), :])
                dk_scr[p] += dot_nn(jnp.concatenate(dscores, axis=0), qkv_ref[p, pl.ds(at, ROWS), :])

        @pl.when(plain)
        def _():
            gradients(lambda h, raw: raw + tiles[1, 0, h, :1, :1].astype(F32))

        @pl.when(jnp.logical_not(plain))
        def _():
            q_row = at + iota((1, ROWS), 1)
            masked = jnp.where((k_seg == seg_of(q_row, ends)) & (k_row <= q_row), 0.0, NEG)
            tile = jnp.maximum(2 - (i - chip), 0)
            gradients(lambda h, raw: raw + (tiles[1, tile, h].astype(F32) + masked))

        return 0

    lax.fori_loop(chip, stop, block, 0)
    dqkv_scr[:, :HALF] = dq_ref[...]
    for p in range(PAIRS):
        dqkv_scr[:, HALF + 128 * p : HALF + 128 * p + 128] = join_pair(dk_scr[p]).astype(BF16)
        dqkv_scr[:, 2 * HALF + 128 * p : 2 * HALF + 128 * p + 128] = join_pair(dv_scr[p]).astype(BF16)
    e_scr[...] = dot_nt(dqkv_scr[...], w_ref[...])
    keep_ref[...] = e_scr[own_rows(core, half), :]
    send_ref[...] = e_scr[own_rows(1 - core, half), :]
    wide = x_ref[...].astype(F32)
    scaled = wide * rms_inverse(wide)
    h_scr[...] = (scaled * gain_ref[...]).astype(BF16)
    dgain = jnp.sum(e_scr[...] * scaled, axis=0, keepdims=True)
    dgain = jnp.transpose(jnp.where(iota((128, dgain.shape[1]), 0) == 0, dgain, 0.0))
    columns = grads_ref.shape[1]
    grads_ref[:, columns - 128 :] = (small_ref[...] + dgain).astype(BF16)
    step = 256
    for i in range(0, h_scr.shape[1], step):
        grads_ref[i : i + step, : 2 * HALF] = dot_tn(h_scr[:, i : i + step], dqkv_scr[:, HALF:]).astype(BF16)
    give(n_sides, at_ref[2], grads_ref, outs)


def cross_grad_stage_kernel(
    at_ref, len_ref, enc_ref, deal_ref, place_ref,
    e_ref, other_ref, late_ref, gain_ref, cot_ref, co_ref, q_ref, o_ref, lse_ref, kv_ref, wc_ref,
    grad_ref, low_ref, dgain_ref, dq_ref, keep_ref, send_ref, part_ref,
    go_ref, qs, gs, lse_scr, delta_scr, dq_scr, block_scr,
):
    chip, core = at_ref[0], at_ref[1]
    dvalue, dgain = norm_grad(late_ref[...], gain_ref[...], e_ref[...] + other_ref[...])
    dgain_ref[...] = dgain
    grad = cot_ref[...].astype(F32) + dvalue
    grad_ref[...] = grad
    low_ref[...] = grad.astype(BF16)
    go_ref[...] = dot_nt(low_ref[...], co_ref[own_rows(core, HALF), :]).astype(BF16)
    wanted, _, mask = cross_flags(chip, len_ref, enc_ref, deal_ref)
    row_stats(go_ref, o_ref, lse_ref, gs, lse_scr, delta_scr, SUB)
    for p in range(PAIRS):
        qs[p] = split_pair(q_ref[:, lanes_of(p)], SUB)
    dq_scr[...] = jnp.zeros_like(dq_scr)
    half = keep_ref.shape[0] // ROWS

    def gradients(j, rows, masked):
        at = pl.multiple_of(j * KEYS, KEYS)
        raws = [dot_nt(qs[p, rows], kv_ref[p, pl.ds(at, KEYS), :]) for p in range(PAIRS)]
        dprobs = [dot_nt(gs[p, rows], kv_ref[PAIRS + p, pl.ds(at, KEYS), :]) for p in range(PAIRS)]
        for p in range(PAIRS):
            probs = jnp.exp(raws[p] + masked - lse_scr[p, rows, :1])
            ds = (probs * (dprobs[p] - delta_scr[p, rows, :1])).astype(BF16)
            dq_scr[p, rows] += dot_nn(ds, kv_ref[p, pl.ds(at, KEYS), :])
            block_scr[:, lanes_of(p)] += dot_tn(ds, qs[p, rows])
            block_scr[:, lanes_of(PAIRS + p)] += dot_tn(probs.astype(BF16), gs[p, rows])

    def block(j, c):
        at = pl.multiple_of(j * KEYS, KEYS)
        hit = wanted(at, 0, ROWS)

        @pl.when(hit)
        def _():
            block_scr[...] = jnp.zeros_like(block_scr)
            for r in range(ROWS // SUB):

                @pl.when(wanted(at, r * SUB, SUB))
                def _():
                    masked = mask(j, r)
                    gradients(j, stacked(r), jnp.concatenate([masked, masked], axis=0))

        for i in range(KEYS // ROWS):
            place = place_ref[j * (KEYS // ROWS) + i]
            upper = (place >= half).astype(jnp.int32)
            to = pl.ds(pl.multiple_of((place - upper * half) * ROWS, ROWS), ROWS)
            for mine, target in ((True, keep_ref), (False, send_ref)):
                here = (upper == at_ref[3]) == mine

                @pl.when(here & hit)
                def _():
                    target[to, :] = block_scr[i * ROWS : (i + 1) * ROWS, :].astype(BF16)

                @pl.when(here & jnp.logical_not(hit))
                def _():
                    target[to, :] = jnp.zeros((ROWS, 2 * HALF), BF16)

        return c

    lax.fori_loop(0, kv_ref.shape[1] // KEYS, block, 0)
    for p in range(PAIRS):
        dq_ref[:, 128 * p : 128 * p + 128] = join_pair(dq_scr[p], SUB).astype(BF16)
    part_ref[...] = dot_nt(dq_ref[...], wc_ref[:, :HALF])


def self_grad_start_kernel(
    at_ref, e_ref, other_ref, mid_ref, gain_ref, late_grad_ref, so_ref, o_ref, lse_ref,
    grad_ref, low_ref, dgain_ref, go_ref, message_ref,
    stat_scr,
):
    core = at_ref[1]
    dvalue, dgain = norm_grad(mid_ref[...], gain_ref[...], e_ref[...] + other_ref[...])
    dgain_ref[...] = dgain
    grad = late_grad_ref[...] + dvalue
    grad_ref[...] = grad
    low_ref[...] = grad.astype(BF16)
    go_ref[...] = dot_nt(low_ref[...], so_ref[own_rows(core, HALF), :]).astype(BF16)
    half = ROWS // 2
    message_ref[:half, :] = low_ref[own_rows(core, half), :]
    lane = iota((ROWS, 128), 1)
    stat_scr[...] = lse_ref[...]

    def pair(p):
        product = go_ref[:, lanes_of(p)].astype(F32) * o_ref[:, lanes_of(p)]
        for i in range(2):
            part = jnp.where((lane < HEAD_DIM) if i == 0 else (lane >= HEAD_DIM), product, 0.0)
            stat_scr[...] = jnp.where(lane == 8 + 2 * p + i, jnp.sum(part, axis=1, keepdims=True), stat_scr[...])

    each_pair(pair)
    rest = jnp.transpose(stat_scr[...])[:16]
    for part in range(3):
        high = rest.astype(BF16)
        message_ref[half:, part * ROWS : (part + 1) * ROWS] = high
        rest = rest - high.astype(F32)


def projection_grads_kernel(
    n_sides, at_ref, low2_ref, other2_ref, b2_ref, in_ref, dq2_ref, low1_ref, other1_ref, b1_ref, x_ref, gain_ref, dq1_ref, *outs
):
    *outs, out_ref = outs
    core, side = at_ref[1], at_ref[2]
    lanes = pl.ds(pl.multiple_of(core * HALF, 128), HALF)
    for at, own, other, grad in ((0, low2_ref, other2_ref, b2_ref), (2 * HALF, low1_ref, other1_ref, b1_ref)):
        grads = grad[:, lanes]
        for which, part in ((core, own), (1 - core, other)):
            out_ref[own_rows(which, HALF), at : at + HALF] = dot_tn(part[...], grads).astype(BF16)
    out_ref[:, HALF : 2 * HALF] = dot_tn(in_ref[...], dq2_ref[...]).astype(BF16)
    wide = x_ref[...].astype(F32)
    normed = (wide * rms_inverse(wide) * gain_ref[...]).astype(BF16)
    out_ref[:, 3 * HALF :] = dot_tn(normed, dq1_ref[...]).astype(BF16)
    give(n_sides, side, out_ref, outs)


def give(n_sides, side, value, outs):
    if n_sides == 2:
        rows = value.shape[0] // 2
        outs[0][...] = value[own_rows(side, rows), :]
        outs[1][...] = value[own_rows(1 - side, rows), :]
    else:
        outs[0][...] = value[...]


def encoder_grads_kernel(n_sides, at_ref, dkv_ref, e_ref, wc_ref, keep_ref, send_ref, *outs):
    *outs, low_scr, e_scr, grads_ref = outs
    core = at_ref[1]
    half = ROWS // 2
    low_scr[...] = dkv_ref[...].astype(BF16)
    e_scr[...] = dot_nt(low_scr[...], wc_ref[:, HALF:])
    keep_ref[...] = e_scr[own_rows(core, half), :]
    send_ref[...] = e_scr[own_rows(1 - core, half), :]
    grads_ref[...] = dot_tn(e_ref[...], low_scr[...]).astype(BF16)
    give(n_sides, at_ref[2], grads_ref, outs)


def token_grads_kernel(at_ref, e_ref, other_ref, x_ref, gain_ref, grad_ref, out_ref):
    dvalue, _ = norm_grad(x_ref[...].astype(F32), gain_ref[...], e_ref[...] + other_ref[...])
    out_ref[...] = grad_ref[own_rows(at_ref[1], out_ref.shape[0]), :] + dvalue


def finish_late_kernel(count, at_ref, place_ref, own_ref, other_ref, *refs):
    *outs, one, two, three, table, small = refs
    core, place = at_ref[1], place_ref[0]
    rows = own_ref.shape[0] // count
    columns = slice(len(outs) * HALF, len(outs) * HALF + 128)
    for i in range(count):
        part = slice(i * rows, (i + 1) * rows)
        to = pl.ds(pl.multiple_of((place ^ i) * rows, rows), rows)
        for j, out in enumerate(outs):
            lanes = slice(j * HALF, (j + 1) * HALF)
            out[to, own_lanes(core)] = own_ref[part, lanes].astype(F32)
            out[to, own_lanes(1 - core)] = other_ref[part, lanes].astype(F32)
        small[to, :] = own_ref[part, columns].astype(F32) + other_ref[part, columns].astype(F32)
    turned = jnp.transpose(small[...])
    for i, out in enumerate((one, two, three)):
        out[...] = turned[i]
    table[...] = small[: table.shape[0], 3 : 3 + HEADS]


def own_lanes(core):
    return pl.ds(pl.multiple_of(core * HALF, 128), HALF)


def finish_kernel(order, parts_ref, outer_ref, inner_ref, *outs):
    rows = parts_ref.shape[1]
    width = outer_ref.shape[1]
    side = inner_ref.shape[0]
    unit = inner_ref.shape[1] // 4
    for i, (core, place) in enumerate(order):
        at = place * rows
        for half in range(2):
            top = (2 * core + half) * side + at
            outer_ref[top : top + rows, :] = parts_ref[i, :, half * width : (half + 1) * width].astype(F32)
            lanes = slice((2 * half + core) * unit, (2 * half + core + 1) * unit)
            inner_ref[at : at + rows, lanes] = parts_ref[i, :, 2 * width + half * unit : 2 * width + (half + 1) * unit].astype(F32)
    finish_columns_kernel(order, 4 * width, parts_ref, *outs)


def finish_columns_kernel(order, skip, parts_ref, *outs):
    rows = parts_ref.shape[1]
    for i, (core, place) in enumerate(order):
        at = slice(place * rows, (place + 1) * rows)
        for j, out in enumerate(outs):
            columns = slice(skip + j * HALF, skip + (j + 1) * HALF)
            out[at, core * HALF : (core + 1) * HALF] = parts_ref[i, :, columns].astype(F32)


def pack_kernel(groups, core_ref, *refs):
    count = sum(groups)
    ins, outs = list(refs[:count]), refs[count:]
    for size, out in zip(groups, outs):
        at = 0
        for _ in range(size):
            part = ins.pop(0)
            out[:, at : at + part.shape[1]] = part[...].astype(BF16)
            at += part.shape[1]


SMEM = pl.BlockSpec(memory_space=pltpu.SMEM)
VMEM = pl.BlockSpec(memory_space=pltpu.VMEM)


def call(kernel, scalars, arrays, outs, scratch, flops):
    moved = sum(a.size * a.dtype.itemsize for a in arrays) + sum(math.prod(s) * jnp.dtype(d).itemsize for s, d in outs)
    return pl.pallas_call(
        kernel,
        out_shape=[jax.ShapeDtypeStruct(s, d) for s, d in outs],
        in_specs=[SMEM] * len(scalars) + [VMEM] * len(arrays),
        out_specs=[VMEM] * len(outs),
        scratch_shapes=[pltpu.VMEM(s, d) for s, d in scratch],
        compiler_params=pltpu.CompilerParams(vmem_limit_bytes=VMEM_LIMIT),
        cost_estimate=pl.CostEstimate(flops=1, transcendentals=0, bytes_accessed=1),
    )(*scalars, *arrays)


TILES = ((3, LOCAL, ROWS, ROWS), F32)
FAR = ((LOCAL, 8, ROWS), F32)
STACK = ((PAIRS, 2 * ROWS, 128), BF16)
COLUMN = ((PAIRS, 2 * ROWS, 128), F32)
LANE = ((ROWS, 128), F32)


def pack(core, groups):
    flat = [item for group in groups for item in group]
    return pl.pallas_call(
        functools.partial(pack_kernel, [len(g) for g in groups]),
        grid_spec=pltpu.PrefetchScalarGridSpec(
            num_scalar_prefetch=1,
            grid=(1,),
            in_specs=[
                pl.BlockSpec(shape, functools.partial(lambda index, i, c: index(c[0]), index)) for _, shape, index in flat
            ],
            out_specs=[
                pl.BlockSpec((g[0][1][0], sum(s[1] for _, s, _ in g)), lambda i, c: (0, 0)) for g in groups
            ],
        ),
        out_shape=[jax.ShapeDtypeStruct((g[0][1][0], sum(s[1] for _, s, _ in g)), BF16) for g in groups],
        compiler_params=pltpu.CompilerParams(vmem_limit_bytes=VMEM_LIMIT),
    )(core, *(w for w, _, _ in flat))


def swap_core(value):
    return lax.ppermute(value, "core", [(0, 1), (1, 0)])


def gather_fsdp(own):
    count = lax.axis_size("fsdp")
    if count != 2:
        return [lax.all_gather(own, "fsdp", axis=0, tiled=True)]
    return [own, lax.ppermute(own, "fsdp", [(0, 1), (1, 0)])]


CHIPS = ("z", "y")
GROUP = ("z", "y", "core")


def gather_rows(own):
    return lax.all_gather(own, GROUP, axis=0, tiled=True)


def bits_of(axis):
    return range((lax.axis_size(axis) - 1).bit_length())


def swap_bit(value, axis, bit):
    return lax.ppermute(value, axis, [(i, i ^ (1 << bit)) for i in range(lax.axis_size(axis))])


def parted(terms, axis, bit):
    side = (lax.axis_index(axis) >> bit) & 1
    rows = terms[0].shape[0] // 2

    def half(which):
        return [lax.dynamic_slice_in_dim(t, which * rows, rows, 0) for t in terms]

    return half(side), total(half(1 - side)).astype(BF16)


def halve(terms, axis, bit):
    keep, send = parted(terms, axis, bit)
    return keep + [swap_bit(send, axis, bit)]


def total(terms):
    return sum(t.astype(F32) for t in terms[1:]) + terms[0].astype(F32)


def steps_of(*axes):
    return [(axis, bit) for axis in axes for bit in bits_of(axis)]


def scatter(terms, steps):
    for axis, bit in steps:
        terms = halve(terms, axis, bit)
    return terms


def scatter_fsdp(terms):
    return scatter(terms, [("fsdp", bit) for bit in reversed(bits_of("fsdp"))])


def places(steps):
    nz, ny = lax.axis_size("z"), lax.axis_size("y")
    found = []
    for z in range(nz):
        for y in range(ny):
            place = 0
            for axis, bit in steps:
                place = 2 * place + (((z if axis == "z" else y) >> bit) & 1)
            found.append(place)
    return found


def after(value, *earlier):
    return lax.optimization_barrier((value, *earlier))[0]


def on_device(
    tokens, encoded, cotangent, tgt_lengths, enc_lengths, deal,
    ln_self, ln_cross, ln_ffn, bias_table,
    self_query, self_key, self_value, self_output,
    cross_query, cross_key, cross_value, cross_output,
    ffn_inner, ffn_outer,
):
    core = lax.axis_index("core")
    fsdp = lax.axis_index("fsdp")
    n_fsdp = lax.axis_size("fsdp")
    chip = lax.axis_index(CHIPS)
    steps = steps_of("y", "z")
    y_side = (lax.axis_index("y") >> steps[0][1]) & 1
    at = jnp.stack([chip, core, fsdp, y_side]).astype(jnp.int32)
    core_ref = core.reshape(1).astype(jnp.int32)
    rows, width = tokens.shape
    n = 2 * rows * lax.axis_size(CHIPS)
    side = width // n_fsdp
    hidden_half = ffn_inner.shape[1] // 2
    unit = hidden_half // n_fsdp
    wide, flat = ((ROWS, width), F32), ((ROWS, width), BF16)

    def column(weight):
        return (weight, (side, HALF), lambda c: (0, c))

    (qkv_own,) = pack(core_ref, [[column(w) for w in (self_query, self_key, self_value)]])
    w_qkv = gather_fsdp(qkv_own)
    if unit % 128 == 0:
        inner_items = [(ffn_inner, (side, unit), functools.partial(lambda o, c: (0, 2 * o + c), o)) for o in range(n_fsdp)]
    else:
        inner_units = ffn_inner.reshape(side, n_fsdp, 2, unit)
        inner_units = lax.dynamic_index_in_dim(inner_units, core, 2, keepdims=False).reshape(side, hidden_half)
        inner_items = [(inner_units, (side, hidden_half), lambda c: (0, 0))]
    out_own, cross_own, inner_own, outer_own = pack(
        core_ref,
        [
            [column(w) for w in (self_output, cross_output)],
            [column(w) for w in (cross_query, cross_key, cross_value)],
            inner_items,
            [(ffn_outer, (unit, width), lambda c: (c, 0))],
        ],
    )
    w_out = gather_fsdp(out_own)
    w_cross = gather_fsdp(cross_own)
    inner_own, outer_own = after((inner_own, outer_own), w_cross[-1])
    w_inner, w_outer = gather_fsdp(inner_own), gather_fsdp(outer_own)
    w_out_mate = [swap_core(w) for w in w_out]
    cot_mate = swap_core(cotangent)

    small = jnp.concatenate([ln_self, ln_cross, ln_ffn, bias_table.reshape(-1)], axis=0).astype(BF16)[None]
    small = gather_fsdp(small)
    if len(small) == 2:
        small = jnp.where(fsdp == 0, jnp.concatenate(small, axis=0), jnp.concatenate(small[::-1], axis=0))
    else:
        small = small[0]
    gain_self, gain_cross, gain_ffn = (
        small[:, i * side : (i + 1) * side].reshape(1, width).astype(F32) for i in range(3)
    )
    table = small[:, 3 * side :].reshape(BUCKETS, HEADS)
    table = lax.dynamic_slice_in_dim(table, core * LOCAL, LOCAL, 1).astype(F32)
    onehots = np.concatenate([QK_ONEHOT, KQ_ONEHOT], axis=0)
    biases = jnp.einsum("bh,tb->ht", table, onehots, precision=lax.Precision.HIGHEST)
    biases = jnp.pad(biases.reshape(LOCAL, 2, 2 * ROWS).swapaxes(0, 1), ((0, 0), (0, 2), (0, 0)))
    (tiles,) = call(tiles_kernel, (), (biases.reshape(16, 2 * ROWS),), [((2, *TILES[0]), BF16)], [], 1)

    xe = gather_rows(jnp.concatenate([tokens, encoded], axis=1))
    qkv, w_qkv, attn_self, low_self, lse_self = call(
        functools.partial(self_stage_kernel, len(w_qkv)), (at, tgt_lengths), (xe, gain_self, tiles, *w_qkv),
        [((3 * PAIRS, n, 128), BF16), ((width, 3 * HALF), BF16), ((ROWS, HALF), F32), ((ROWS, HALF), BF16), LANE],
        ATTEND(n),
        2 * n * width * 3 * HALF + 4 * ROWS * n * HALF,
    )
    low_self_other = swap_core(low_self)

    x_mid, in_cross, q_cross, kv_cross, attn_cross, low_cross, lse_cross, w_so, w_co, w_cross = call(
        functools.partial(cross_stage_kernel, len(w_out)), (at, tgt_lengths, enc_lengths, deal),
        (xe, gain_cross, low_self, low_self_other, *w_out, *w_out_mate, *w_cross),
        [
            wide, flat, ((ROWS, HALF), BF16), ((2 * PAIRS, n, 128), BF16), ((ROWS, HALF), F32), ((ROWS, HALF), BF16), LANE,
            ((width, width), BF16), ((width, width), BF16), ((width, 3 * HALF), BF16),
        ],
        ATTEND(n),
        2 * n * width * 2 * HALF + 4 * ROWS * n * HALF,
    )
    low_cross_other = swap_core(low_cross)

    half_rows = ((rows, width), F32)
    x_late, in_ffn, hidden, d_pre, cot, out_keep, out_send, e_ffn = call(
        functools.partial(ffn_stage_kernel, len(w_inner)), (at,),
        (x_mid, gain_ffn, low_cross, low_cross_other, w_co, cotangent, cot_mate, *w_inner, *w_outer),
        [wide, flat, ((ROWS, hidden_half), BF16), ((ROWS, hidden_half), BF16), flat, half_rows, half_rows, wide],
        [((width, hidden_half), BF16), ((hidden_half, width), BF16), wide],
        8 * ROWS * width * hidden_half,
    )
    e_ffn_other = swap_core(e_ffn)
    output = out_keep + swap_core(out_send)

    place = places(steps)
    place_ref = jnp.asarray(np.array(place, np.int32))
    nz, ny = lax.axis_size("z"), lax.axis_size("y")
    y_place = [p // nz for p in place[:ny]]
    key_place_ref = jnp.asarray(np.array([y_place[y] * nz + z for z in range(nz) for y in range(ny)], np.int32))
    grad_late, late_low, d_gain_ffn, dq_cross, dkv_keep, dkv_send, e_cross = call(
        cross_grad_stage_kernel, (at, tgt_lengths, enc_lengths, deal, key_place_ref),
        (e_ffn, e_ffn_other, x_late, gain_ffn, cot, w_co, q_cross, attn_cross, lse_cross, kv_cross, w_cross),
        [wide, flat, ((1, width), F32), ((ROWS, HALF), BF16), ((n // 2, 2 * HALF), BF16), ((n // 2, 2 * HALF), BF16), wide],
        [((ROWS, HALF), BF16), STACK, STACK, COLUMN, COLUMN, COLUMN, ((KEYS, 2 * HALF), F32)],
        10 * ROWS * n * HALF,
    )
    e_cross_other = swap_core(e_cross)
    dkv_got = swap_bit(dkv_send, *steps[0])

    grad_mid, mid_low, d_gain_cross, go_self, message = call(
        self_grad_start_kernel, (at,), (e_cross, e_cross_other, x_mid, gain_cross, grad_late, w_so, attn_self, lse_self),
        [wide, flat, ((1, width), F32), ((ROWS, HALF), BF16), ((rows + 16, width), BF16)], [LANE],
        2 * ROWS * width * HALF,
    )
    ffn_out = (
        [((side, 4 * width), BF16), ((side, 4 * width), BF16)]
        if n_fsdp == 2
        else [((hidden_half, width), F32), ((width, hidden_half), F32)]
    )
    first = call(
        functools.partial(ffn_grads_kernel, n_fsdp), (at,), (hidden, cot, in_ffn, after(d_pre, message)), ffn_out, [],
        4 * ROWS * width * hidden_half,
    )
    if n_fsdp == 2:
        first_other = lax.ppermute(first[1], "fsdp", [(0, 1), (1, 0)])
        go_self = after(go_self, first[1])
    message = lax.all_gather(message, GROUP, axis=0)
    x_chip = lax.dynamic_slice(xe, (chip * ROWS, 0), (ROWS, width))
    e_chip = lax.dynamic_slice(xe, (chip * ROWS, width), (ROWS, width))
    dq_self, dist = call(
        self_query_grad_kernel, (at, tgt_lengths), (tiles, qkv, go_self, attn_self, lse_self),
        [((ROWS, HALF), BF16), ((8, 2 * ROWS), F32)],
        [STACK, STACK, COLUMN, COLUMN, COLUMN, TILES, FAR],
        6 * ROWS * n * HALF,
    )
    def given(columns):
        return [((width // 2, columns), BF16)] * 2 if n_fsdp == 2 else [((width, columns), BF16)]

    def over_fsdp(parts):
        if n_fsdp == 2:
            return [parts[0], lax.ppermute(parts[1], "fsdp", [(0, 1), (1, 0)])]
        return scatter_fsdp(parts)

    second = call(
        functools.partial(projection_grads_kernel, n_fsdp), (at,),
        (low_cross, low_cross_other, late_low, in_cross, dq_cross, low_self, low_self_other, mid_low, x_chip, gain_self, dq_self),
        given(4 * HALF), [((width, 4 * HALF), BF16)], 8 * ROWS * width * HALF,
    )
    d_table = jnp.einsum("ht,tb->bh", dist[:LOCAL], QK_ONEHOT, precision=lax.Precision.HIGHEST)
    d_table = jnp.zeros((BUCKETS, 2, LOCAL), F32).at[:, core].set(d_table).reshape(n_fsdp, -1, HEADS)
    d_table = jnp.pad(d_table, ((0, 0), (0, side - d_table.shape[1]), (0, 0))).reshape(width, HEADS)
    none = jnp.zeros((width, 1), F32)
    small = [none, 0.5 * d_gain_cross.reshape(width, 1), 0.5 * d_gain_ffn.reshape(width, 1), d_table]
    small = jnp.pad(jnp.concatenate(small, axis=1), ((0, 0), (0, 128 - 3 - HEADS)))

    if n_fsdp == 2:
        first = [first[0], first_other]
    else:
        outer = first[0].reshape(n_fsdp, 2, side, width)
        first = jnp.concatenate([outer[:, 0], outer[:, 1], first[1].reshape(n_fsdp, side, hidden_half)], axis=2)
        first = scatter_fsdp([first.reshape(width, -1)])
    *y_steps, z_near, z_far = steps
    dkv_cross = scatter(after([dkv_keep, dkv_got], second[-1]), y_steps[1:])
    dkv_cross = total(dkv_cross).astype(BF16)
    first = after(first, dkv_cross)
    second = over_fsdp(after(second, first[-1]))
    first_keep, first_sent = parted(first, *y_steps[0])
    first_got = swap_bit(first_sent, *y_steps[0])
    dkv_cross = lax.psum_scatter(dkv_cross, "z", scatter_dimension=0, tiled=True)

    e_keep, e_send, *fourth = call(
        functools.partial(self_key_stage_kernel, n_fsdp), (at, tgt_lengths),
        (tiles, qkv, after(message, first_sent), w_so, dq_self, w_qkv, x_chip, gain_self, small),
        [half_rows, half_rows, *given(2 * HALF + 128)],
        [
            ((PAIRS, n, 128), BF16), ((n // ROWS, 16, ROWS), F32), STACK, STACK, COLUMN, COLUMN,
            ((ROWS, 3 * HALF), BF16), flat, wide, ((width, 2 * HALF + 128), BF16),
        ],
        8 * ROWS * n * HALF,
    )
    fourth_sent = fourth[-1]
    fourth = over_fsdp(fourth)
    first = scatter(first_keep + [after(first_got, fourth_sent)], y_steps[1:])
    first_keep, first_sent = parted(first, *z_near)
    first_got = swap_bit(first_sent, *z_near)
    second, fourth = after((second, fourth), first_sent)
    second = jnp.concatenate([total(second), total(fourth)], axis=1).astype(BF16)
    second_keep, second_sent = parted([second], *y_steps[0])
    second_got = swap_bit(second_sent, *y_steps[0])
    enc_keep, enc_send, *third = call(
        functools.partial(encoder_grads_kernel, n_fsdp), (at,), (after(dkv_cross, second_sent), e_chip, w_cross),
        [half_rows, half_rows, *given(2 * HALF)],
        [((ROWS, 2 * HALF), BF16), wide, ((width, 2 * HALF), BF16)], 8 * ROWS * width * HALF,
    )
    third_sent = third[-1]
    third = over_fsdp(third)
    first_keep, first_sent = parted(first_keep + [after(first_got, third_sent)], *z_far)
    first_got = swap_bit(first_sent, *z_far)
    (grad_tokens,) = call(
        token_grads_kernel, (at,), (e_keep, swap_core(after(e_send, first_sent)), tokens, gain_self, grad_mid),
        [half_rows], [], 10 * rows * width,
    )
    enc_grad = enc_keep + swap_core(after(enc_send, first_sent))

    second = scatter(second_keep + [after(second_got, grad_tokens, enc_grad)], y_steps[1:])
    second_keep, second_sent = parted(second, *z_near)
    second_got = swap_bit(second_sent, *z_near)
    late_keep, late_sent = parted(after(third, second_sent), *y_steps[0])
    late_got = swap_bit(late_sent, *y_steps[0])
    first = total(first_keep + [after(first_got, late_sent)]).astype(BF16)
    second_keep, second_sent = parted(second_keep + [after(second_got, first)], *z_far)
    second_got = swap_bit(second_sent, *z_far)
    late = scatter(late_keep + [after(late_got, second_sent)], y_steps[1:])
    late_keep, late_sent = parted(late, *z_near)
    late_got = swap_bit(late_sent, *z_near)
    second = total(second_keep + [after(second_got, late_sent)]).astype(BF16)
    early = lax.all_gather(jnp.concatenate([first, second[:, : 4 * HALF]], axis=1), GROUP, axis=0)
    late = total(halve(late_keep + [after(late_got, second)], *z_far)).astype(BF16)
    late = jnp.concatenate([late, second[:, 4 * HALF :]], axis=1)
    for axis, bit in reversed(steps):
        late = jnp.concatenate([late, swap_bit(late, axis, bit)], axis=0)
    late_other = swap_core(late)
    early = after(early, late_other)

    matrix = ((side, width), F32)
    own_place = place_ref[chip].reshape(1)
    if side // len(place) % 8 == 0:
        g_ck, g_cv, g_sk, g_sv, *gains, g_table = call(
            functools.partial(finish_late_kernel, len(place)), (at, own_place), (late, late_other),
            [matrix] * 4 + [((side,), F32)] * 3 + [(bias_table.shape, F32)], [((side, 128), F32)], 8 * side * width,
        )
    else:
        blocks = jnp.stack([late, late_other]).reshape(2, len(place), side // len(place), -1)
        blocks = jnp.take(blocks, own_place[0] ^ jnp.arange(len(place), dtype=jnp.int32), axis=1)
        blocks = jnp.where(core == 0, blocks, blocks[::-1]).astype(F32).reshape(2, side, -1)
        g_ck, g_cv, g_sk, g_sv = (
            jnp.swapaxes(blocks[:, :, i : i + HALF], 0, 1).reshape(side, width) for i in range(0, 4 * HALF, HALF)
        )
        small = jnp.sum(blocks[:, :, 4 * HALF :], axis=0)
        gains = [small[:, i] for i in range(3)]
        g_table = small[: bias_table.shape[0], 3 : 3 + HEADS]
    order = [(c, p) for p in place for c in range(2)]
    if n_fsdp == 2:
        g_outer, g_inner, g_co, g_cq, g_so, g_sq = call(
            functools.partial(finish_kernel, order), (), (early,),
            [(ffn_outer.shape, F32), (ffn_inner.shape, F32), *[matrix] * 4], [], 8 * side * width,
        )
    else:
        sources = np.argsort([2 * p + c for c, p in order])
        pair = jnp.swapaxes(early[sources].reshape(len(place), 2, -1, early.shape[2]), 0, 1)
        pair = pair.reshape(2, side, -1).astype(F32)
        g_outer = pair[:, :, : 2 * width].reshape(2, side, 2, width)
        g_outer = jnp.swapaxes(g_outer, 1, 2).reshape(ffn_outer.shape)
        g_inner = jnp.transpose(pair[:, :, 2 * width : 4 * width].reshape(2, side, n_fsdp, unit), (1, 2, 0, 3))
        g_inner = g_inner.reshape(ffn_inner.shape)
        g_co, g_cq, g_so, g_sq = call(
            functools.partial(finish_columns_kernel, order, 4 * width), (), (early,), [matrix] * 4, [], 8 * side * width
        )

    return (
        output, grad_tokens, enc_grad,
        *gains, g_table,
        g_sq, g_sk, g_sv, g_so, g_cq, g_ck, g_cv, g_co, g_inner, g_outer,
    )


def solution(mesh):
    n_ctx, n_fsdp = mesh.shape["ctx"], mesh.shape["fsdp"]
    n_z = 4
    grid = Mesh(mesh.devices.reshape(n_z, n_ctx // (2 * n_z), 2, n_fsdp), ("z", "y", "core", "fsdp"))
    by_rows = P(("fsdp", "z", "y", "core"), None)
    split = P("fsdp", None)
    vector = P("fsdp")
    in_specs = (by_rows,) * 3 + (split,) * 3 + (vector,) * 3 + (split,) * 11
    out_specs = (by_rows,) * 3 + (vector,) * 3 + (split,) * 11
    return jax.shard_map(on_device, mesh=grid, in_specs=in_specs, out_specs=out_specs, check_vma=False)
```

profile of v0, /device:TPU:0, one launch (start us, length us, event | category | flops | bytes accessed | tf_op | source)
XLA Modules:
  0.0 422.5 jit_solution(808409010154196791)
XLA Ops:
  9.2 5.3 %shard_map.362 = (bf16[384,768]{1,0:T(8,128)(2,1)}, bf16[384,1152]{1,0:T(8,128)(2,1)}, bf16[384,1536]{1,0:T(8,128)(2,1)}, bf16[768,768]{1,0:T(8,128)(2,1)}) custom-call(s32[1]{0:T(128)} %bitcast.1.core_ref, f32[384,768]{1,0:T(8,128)} %refs_0_.3, f32[384,768]{1,0:T(8,128)} %refs_1_.3, f32[384,768]{1,0:T(8,128)} %refs_2_.3, f32[384,768]{1,0:T(8,128)} %refs_3_.1, ...), custom_call_target="tpu_custom_call" | custom-call | tf_op jit(solution)/shard_map/pallas_call | solution.py:867
  22.4 15.7 %collective-permute-done.6.refs_5_ = bf16[384,1152]{1,0:T(8,128)(2,1)S(1)} collective-permute-done((bf16[384,1152]{1,0:T(8,128)(2,1)}, bf16[384,1152]{1,0:T(8,128)(2,1)S(1)}, u32[]{:S(2)}, u32[]{:S(2)}) %collective-permute-start.6) | collective-permute-done | bytes 884768 | tf_op jit(solution)/shard_map/ppermute | solution.py:892
  41.0 9.8 %collective-permute-done = bf16[1,1344]{1,0:T(2,128)(2,1)S(1)} collective-permute-done((bf16[1,1344]{1,0:T(2,128)(2,1)S(1)}, bf16[1,1344]{1,0:T(2,128)(2,1)S(1)}, u32[]{:S(2)}, u32[]{:S(2)}) %collective-permute-start) | collective-permute-done | bytes 2720 | tf_op jit(solution)/shard_map/ppermute | solution.py:892
  58.4 3.8 shard_map.359.tiles
  62.8 7.1 %collective-permute-done.1.refs_1_ = bf16[384,1152]{1,0:T(8,128)(2,1)} collective-permute-done((bf16[384,1152]{1,0:T(8,128)(2,1)}, bf16[384,1152]{1,0:T(8,128)(2,1)}, u32[]{:S(2)}, u32[]{:S(2)}) %collective-permute-start.1) | collective-permute-done | bytes 884768 | tf_op jit(solution)/shard_map/ppermute | solution.py:892
  69.9 5.6 %all-gather.6.cloned.1.call-done.xe_ref = bf16[2048,1536]{1,0:T(8,128)(2,1)} async-done(((bf16[128,1536]{1,0:T(8,128)(2,1)}), bf16[2048,1536]{1,0:T(8,128)(2,1)}) %all-gather.6.cloned.1.call-update) | async-done | bytes 6291472 | tf_op jit(solution)/shard_map/all_gather | solution.py:900
  75.5 14.3 %shard_map.361 = (bf16[9,2048,128]{2,1,0:T(8,128)(2,1)}, bf16[768,1152]{1,0:T(8,128)(2,1)}, f32[256,384]{1,0:T(8,128)}, bf16[256,384]{1,0:T(8,128)(2,1)}, f32[256,128]{1,0:T(8,128)}) custom-call(s32[4]{0:T(128)} %pad_add_fusion.at_ref, s32[1,6]{1,0:T(1,128)} %len_ref.9, bf16[2048,1536]{1,0:T(8,128)(2,1)} %all-gather.6.cloned.1.call-done.xe_ref, ...), custom_call_target="tpu_custom_call" | custom-call | flops 1 | bytes 1 | tf_op jit(solution)/shard_map/pallas_call | solution.py:847
  92.1 16.2 %shard_map.363 = (f32[256,768]{1,0:T(8,128)}, bf16[256,768]{1,0:T(8,128)(2,1)}, bf16[256,384]{1,0:T(8,128)(2,1)}, bf16[6,2048,128]{2,1,0:T(8,128)(2,1)}, f32[256...) custom-call(s32[4]{0:T(128)} %pad_add_fusion.at_ref, ...), custom_call_target="tpu_custom_call" | custom-call | flops 1 | bytes 1 | tf_op jit(solution)/shard_map/pallas_call | solution.py:847
  109.2 10.4 %collective-permute-done.10.refs_3_ = bf16[768,768]{1,0:T(8,128)(2,1)} collective-permute-done((bf16[768,768]{1,0:T(8,128)(2,1)S(1)}, bf16[768,768]{1,0:T(8,128)(2,1)}, u32[]{:S(2)}, u32[]{:S(2)}) %collective-permute-start.10) | collective-permute-done | bytes 1179680 | tf_op jit(solution)/shard_map/ppermute | solution.py:892
  120.3 8.7 %shard_map.364 = (f32[256,768]{1,0:T(8,128)}, bf16[256,768]{1,0:T(8,128)(2,1)}, bf16[256,1536]{1,0:T(8,128)(2,1)}, bf16[256,1536]{1,0:T(8,128)(2,1)}, bf16[256,7...) custom-call(s32[4]{0:T(128)} %pad_add_fusion.at_ref, ...), custom_call_target="tpu_custom_call" | custom-call | flops 1 | bytes 1 | tf_op jit(solution)/shard_map/pallas_call | solution.py:847
  132.4 13.4 %shard_map.365 = (f32[256,768]{1,0:T(8,128)}, bf16[256,768]{1,0:T(8,128)(2,1)}, f32[1,768]{1,0:T(1,128)}, bf16[256,384]{1,0:T(8,128)(2,1)}, bf16[1024,768]{1,0:T...) custom-call(s32[4]{0:T(128)} %pad_add_fusion.at_ref, s32[1,6]{1,0:T(1,128)} %len_ref.9, s32[1,6]{1,0:T(1,128)} %enc_ref.3, ...), custom_call_target="tpu_custom_call" | custom-call | flops 1 | bytes 1 | tf_op jit(solution)/shard_map/pallas_call | solution.py:847
  149.1 4.1 shard_map.366
  153.3 5.7 %shard_map.367 = (bf16[384,3072]{1,0:T(8,128)(2,1)}, bf16[384,3072]{1,0:T(8,128)(2,1)}) custom-call(s32[4]{0:T(128)} %pad_add_fusion.at_ref, bf16[256,1536]{1,0:T(8,128)(2,1)} %get-tuple-element.152.hid_ref, bf16[256,768]{1,0:T(8,128)(2,1)} %get-tuple-element.140.cot_ref, bf16[256,768]{1,0:T(8,128)(2,1)} %get-tuple-element.153.in_ref, ...), custom_call_target="tpu_custom_call" | custom-call | flops 1 | bytes 1 | tf_op jit(solution)/shard_map/pallas_call | solution.py:847
  159.0 7.1 %collective-permute-start.14 = (bf16[384,3072]{1,0:T(8,128)(2,1)}, bf16[384,3072]{1,0:T(8,128)(2,1)}, u32[]{:S(2)}, u32[]{:S(2)}) collective-permute-start(bf16[384,3072]{1,0:T(8,128)(2,1)} %get-tuple-element.157), channel_id=1, source_target_pairs={{0,1},{1,0},{2,3},{3,2},{4,5},{5,4},{6,7},{7,6},{8,9},{9,8},{10,11... | collective-permute-start | bytes 7077896 | tf_op jit(solution)/shard_map/ppermute | solution.py:1087
  170.4 9.4 %shard_map.368 = (bf16[256,384]{1,0:T(8,128)(2,1)}, f32[8,512]{1,0:T(8,128)}) custom-call(s32[4]{0:T(128)} %pad_add_fusion.at_ref, s32[1,6]{1,0:T(1,128)} %len_ref.9, bf16[2,3,6,256,256]{4,3,2,1,0:T(8,128)(2,1)} %shard_map.359.tiles, bf16[9,2048,128]{2,1,0:T(8,128)(2,1)} %get-tuple-element.137.qkv_ref, bf16[256,384]{1,0:T(8,128)(2,1)} %get-tuple-element.165.go_ref, ...), custom_call_target="tpu_custom_call" | custom-call | flops 1 | bytes 1 | tf_op jit(solution)/shard_map/pallas_call | solution.py:847
  179.8 4.4 %shard_map.369 = (bf16[384,1536]{1,0:T(8,128)(2,1)}, bf16[384,1536]{1,0:T(8,128)(2,1)}) custom-call(s32[4]{0:T(128)} %pad_add_fusion.at_ref, bf16[256,384]{1,0:T(8,128)(2,1)} %get-tuple-element.129.low_ref.low2_ref, bf16[256,384]{1,0:T(8,128)(2,1)} %copy-done.12, bf16[256,768]{1,0:T(8,128)(2,1)} %get-tuple-element.160.b2_ref, ...), custom_call_target="tpu_custom_call" | custom-call | flops 1 | bytes 1 | tf_op jit(solution)/shard_map/pallas_call | solution.py:847
  184.2 30.1 %collective-permute-done.15 = bf16[1024,768]{1,0:T(8,128)(2,1)S(1)} collective-permute-done((bf16[1024,768]{1,0:T(8,128)(2,1)}, bf16[1024,768]{1,0:T(8,128)(2,1)S(1)}, u32[]{:S(2)}, u32[]{:S(2)}) %collective-permute-start.15) | collective-permute-done | bytes 1572896 | tf_op jit(solution)/shard_map/ppermute | solution.py:908
  215.4 3.1 add_convert_fusion
  226.1 20.7 %shard_map.370 = (f32[128,768]{1,0:T(8,128)}, f32[128,768]{1,0:T(8,128)}, bf16[384,896]{1,0:T(8,128)(2,1)}, bf16[384,896]{1,0:T(8,128)(2,1)}) custom-call(s32[4]{0:T(128)} %pad_add_fusion.at_ref, s32[1,6]{1,0:T(1,128)} %len_ref.9, bf16[2,3,6,256,256]{4,3,2,1,0:T(8,128)(2,1)} %shard_map.359.tiles, bf16[9,2048,128]{2,1,0:T(8,128)(2,1)} %get-tuple-element.137.qkv_ref, ...), custom_call_target="tpu_custom_call" | custom-call | flops 1 | bytes 1 | tf_op jit(solution)/shard_map/pallas_call | solution.py:847
  253.2 12.7 %collective-permute-done.19 = bf16[384,896]{1,0:T(8,128)(2,1)} collective-permute-done((bf16[384,896]{1,0:T(8,128)(2,1)}, bf16[384,896]{1,0:T(8,128)(2,1)}, u32[]{:S(2)}, u32[]{:S(2)}) %collective-permute-start.19) | collective-permute-done | bytes 688160 | tf_op jit(solution)/shard_map/ppermute | solution.py:1103
  270.1 3.7 shard_map.371
  285.3 5.3 %collective-permute-done.23 = bf16[192,2432]{1,0:T(8,128)(2,1)S(1)} collective-permute-done((bf16[192,2432]{1,0:T(8,128)(2,1)}, bf16[192,2432]{1,0:T(8,128)(2,1)S(1)}, u32[]{:S(2)}, u32[]{:S(2)}) %collective-permute-start.23) | collective-permute-done | bytes 933920 | tf_op jit(solution)/shard_map/ppermute | solution.py:908
  296.5 7.4 %collective-permute-done.25 = bf16[96,2432]{1,0:T(8,128)(2,1)S(1)} collective-permute-done((bf16[96,2432]{1,0:T(8,128)(2,1)S(1)}, bf16[96,2432]{1,0:T(8,128)(2,1)S(1)}, u32[]{:S(2)}, u32[]{:S(2)}) %collective-permute-start.25) | collective-permute-done | bytes 466976 | tf_op jit(solution)/shard_map/ppermute | solution.py:908
  306.7 10.5 %collective-permute-done.28 = bf16[48,2432]{1,0:T(8,128)(2,1)S(1)} collective-permute-done((bf16[48,2432]{1,0:T(8,128)(2,1)S(1)}, bf16[48,2432]{1,0:T(8,128)(2,1)S(1)}, u32[]{:S(2)}, u32[]{:S(2)}) %collective-permute-start.28) | collective-permute-done | bytes 233504 | tf_op jit(solution)/shard_map/ppermute | solution.py:908
  318.3 5.1 %collective-permute-done.27 = bf16[96,768]{1,0:T(8,128)(2,1)S(1)} collective-permute-done((bf16[96,768]{1,0:T(8,128)(2,1)S(1)}, bf16[96,768]{1,0:T(8,128)(2,1)S(1)}, u32[]{:S(2)}, u32[]{:S(2)}) %collective-permute-start.27) | collective-permute-done | bytes 147488 | tf_op jit(solution)/shard_map/ppermute | solution.py:908
  326.2 4.4 %collective-permute-done.29 = bf16[48,768]{1,0:T(8,128)(2,1)S(1)} collective-permute-done((bf16[48,768]{1,0:T(8,128)(2,1)S(1)}, bf16[48,768]{1,0:T(8,128)(2,1)S(1)}, u32[]{:S(2)}, u32[]{:S(2)}) %collective-permute-start.29) | collective-permute-done | bytes 73760 | tf_op jit(solution)/shard_map/ppermute | solution.py:908
  334.0 14.7 %collective-permute-done.30 = bf16[48,1664]{1,0:T(8,128)(2,1)S(1)} collective-permute-done((bf16[48,1664]{1,0:T(8,128)(2,1)S(1)}, bf16[48,1664]{1,0:T(8,128)(2,1)S(1)}, u32[]{:S(2)}, u32[]{:S(2)}) %collective-permute-start.30) | collective-permute-done | bytes 159776 | tf_op jit(solution)/shard_map/ppermute | solution.py:908
  350.1 7.2 %collective-permute-done.31 = bf16[96,1664]{1,0:T(8,128)(2,1)S(1)} collective-permute-done((bf16[96,1664]{1,0:T(8,128)(2,1)S(1)}, bf16[96,1664]{1,0:T(8,128)(2,1)S(1)}, u32[]{:S(2)}, u32[]{:S(2)}) %collective-permute-start.31) | collective-permute-done | bytes 319520 | tf_op jit(solution)/shard_map/ppermute | solution.py:908
  360.4 27.2 %collective-permute-done.32 = bf16[192,1664]{1,0:T(8,128)(2,1)S(1)} collective-permute-done((bf16[192,1664]{1,0:T(8,128)(2,1)S(1)}, bf16[192,1664]{1,0:T(8,128)(2,1)S(1)}, u32[]{:S(2)}, u32[]{:S(2)}) %collective-permute-start.32) | collective-permute-done | bytes 639008 | tf_op jit(solution)/shard_map/ppermute | solution.py:908
  393.0 5.0 %shard_map.373 = (f32[384,768]{1,0:T(8,128)}, f32[384,768]{1,0:T(8,128)}, f32[384,768]{1,0:T(8,128)}, f32[384,768]{1,0:T(8,128)}, f32[384]{0:T(512)}, /*index=5*/f32[384]{0:T(512)}, f32[384]{0:T(512)}, f32[16,12]{1,0:T(8,128)}) custom-call(s32[4]{0:T(128)} %pad_add_fusion.at_ref, s32[1]{0:T(128)} %dynamic_slice.183.place_ref, bf16[384,1664]{1,0:T(8,128)(2,1)} %copy-done, ...), custom_call_target="tpu_custom_call" | custom-call | flops 1 | bytes 1 | tf_op jit(solution)/shard_map/pallas_call | solution.py:847
  398.0 9.2 %all-gather.10.cloned.1.call-done = bf16[768,4608]{1,0:T(8,128)(2,1)} async-done(((bf16[48,4608]{1,0:T(8,128)(2,1)}), bf16[768,4608]{1,0:T(8,128)(2,1)}) %all-gather.10.cloned.1.call-update) | async-done | bytes 7077904 | tf_op jit(solution)/shard_map/all_gather | solution.py:1179
  407.2 8.4 %shard_map.374 = (f32[1536,768]{1,0:T(8,128)}, f32[384,3072]{1,0:T(8,128)}, f32[384,768]{1,0:T(8,128)}, f32[384,768]{1,0:T(8,128)}, f32[384,768]{1,0:T(8,128)}, /*index=5*/f32[384,768]{1,0:T(8,128)}) custom-call(bf16[16,48,4608]{2,1,0:T(8,128)(2,1)} %bitcast.45), custom_call_target="tpu_custom_call" | custom-call | flops 1 | bytes 1 | tf_op jit(solution)/shard_map/pallas_call | solution.py:847
  (187 shorter events, 92.4 us)
Async XLA Ops:
  7.2 68.3 %all-gather.6.cloned.1.call-start = ((), (), s32[]{:S(2)}) async-start(), calls=%async_computation.1 | async-start | bytes 6684672 | tf_op jit(solution)/shard_map/all_gather | solution.py:900
  9.1 217.0 %all-gather.8.cloned.1.call-start = ((), (), s32[]{:S(2)}) async-start(), calls=%async_computation.3 | async-start | bytes 3760128 | tf_op jit(solution)/shard_map/all_gather | solution.py:1089
  14.4 23.6 %collective-permute-start.6 = (bf16[384,1152]{1,0:T(8,128)(2,1)}, bf16[384,1152]{1,0:T(8,128)(2,1)S(1)}, u32[]{:S(2)}, u32[]{:S(2)}) collective-permute-start(bf16[384,1152]{1,0:T(8,128)(2,1)} %get-tuple-element.127.refs_4_), channel_id=1, source_target_pairs={{0,1},{1,0},{2,3},{3,2},{4,5},{5,4},{6,7},{7,6},{8,9},{9,8},{10,11... | collective-permute-start | bytes 2654216 | tf_op jit(solution)/shard_map/ppermute | solution.py:892
  17.4 39.7 %collective-permute-start.3 = (bf16[384,768]{1,0:T(8,128)(2,1)}, bf16[384,768]{1,0:T(8,128)(2,1)}, u32[]{:S(2)}, u32[]{:S(2)}) collective-permute-start(bf16[384,768]{1,0:T(8,128)(2,1)} %get-tuple-element.126.refs_0_), channel_id=1, source_target_pairs={{0,1},{1,0},{2,3},{3,2},{4,5},{5,4},{6,7},{7,6},{8,9},{9,8},{10,11... | collective-permute-start | bytes 1769480 | tf_op jit(solution)/shard_map/ppermute | solution.py:892
  17.7 33.2 %collective-permute-start = (bf16[1,1344]{1,0:T(2,128)(2,1)S(1)}, bf16[1,1344]{1,0:T(2,128)(2,1)S(1)}, u32[]{:S(2)}, u32[]{:S(2)}) collective-permute-start(bf16[1,1344]{1,0:T(2,128)(2,1)S(1)} %constant_dynamic-update-slice_fusion), channel_id=1, source_target_pairs={{0,1},{1,0},{2,3},{3,2},{4,5},{5,4},{6,7},{7,6},{8,9},{9,8},{10,11... | collective-permute-start | bytes 8072 | tf_op jit(solution)/shard_map/ppermute | solution.py:892
  19.7 70.9 %collective-permute-start.4 = (bf16[384,768]{1,0:T(8,128)(2,1)}, bf16[384,768]{1,0:T(8,128)(2,1)}, u32[]{:S(2)}, u32[]{:S(2)}) collective-permute-start(bf16[384,768]{1,0:T(8,128)(2,1)} %get-tuple-element.126.refs_0_), channel_id=1, source_target_pairs={{0,2},{2,0},{1,3},{3,1},{4,6},{6,4},{5,7},{7,5},{8,10},{10,8},{9,1... | collective-permute-start | bytes 1769480 | tf_op jit(solution)/shard_map/ppermute | solution.py:885
  22.2 47.7 %collective-permute-start.1 = (bf16[384,1152]{1,0:T(8,128)(2,1)}, bf16[384,1152]{1,0:T(8,128)(2,1)}, u32[]{:S(2)}, u32[]{:S(2)}) collective-permute-start(bf16[384,1152]{1,0:T(8,128)(2,1)} %shard_map.360.refs_0_), channel_id=1, source_target_pairs={{0,1},{1,0},{2,3},{3,2},{4,5},{5,4},{6,7},{7,6},{8,9},{9,8},{10,11... | collective-permute-start | bytes 2654216 | tf_op jit(solution)/shard_map/ppermute | solution.py:892
  39.0 70.2 %collective-permute-start.9 = (bf16[384,1536]{1,0:T(8,128)(2,1)S(1)}, bf16[384,1536]{1,0:T(8,128)(2,1)S(1)}, u32[]{:S(2)}, u32[]{:S(2)}) collective-permute-start(bf16[384,1536]{1,0:T(8,128)(2,1)S(1)} %copy-done.6), channel_id=1, source_target_pairs={{0,1},{1,0},{2,3},{3,2},{4,5},{5,4},{6,7},{7,6},{8,9},{9,8},{10,11... | collective-permute-start | bytes 3538952 | tf_op jit(solution)/shard_map/ppermute | solution.py:892
  51.4 68.2 %collective-permute-start.10 = (bf16[768,768]{1,0:T(8,128)(2,1)S(1)}, bf16[768,768]{1,0:T(8,128)(2,1)}, u32[]{:S(2)}, u32[]{:S(2)}) collective-permute-start(bf16[768,768]{1,0:T(8,128)(2,1)S(1)} %copy-done.7), channel_id=1, source_target_pairs={{0,1},{1,0},{2,3},{3,2},{4,5},{5,4},{6,7},{7,6},{8,9},{9,8},{10,11... | collective-permute-start | bytes 3538952 | tf_op jit(solution)/shard_map/ppermute | solution.py:892
  57.1 33.8 %collective-permute-start.5 = (bf16[384,768]{1,0:T(8,128)(2,1)}, bf16[384,768]{1,0:T(8,128)(2,1)}, u32[]{:S(2)}, u32[]{:S(2)}) collective-permute-start(bf16[384,768]{1,0:T(8,128)(2,1)} %collective-permute-done.3.refs_1_), channel_id=1, source_target_pairs={{0,2},{2,0},{1,3},{3,1},{4,6},{6,4},{5,7},{7,5},{8,10},{10,8},{9,1... | collective-permute-start | bytes 1769480 | tf_op jit(solution)/shard_map/ppermute | solution.py:885
  90.6 18.6 %collective-permute-start.8 = (bf16[128,768]{1,0:T(8,128)(2,1)S(1)}, bf16[128,768]{1,0:T(8,128)(2,1)S(1)}, u32[]{:S(2)}, u32[]{:S(2)}) collective-permute-start(bf16[128,768]{1,0:T(8,128)(2,1)S(1)} %copy-done.20), channel_id=1, source_target_pairs={{0,2},{2,0},{1,3},{3,1},{4,6},{6,4},{5,7},{7,5},{8,10},{10,8},{9,1... | collective-permute-start | bytes 589832 | tf_op jit(solution)/shard_map/ppermute | solution.py:885
  108.3 11.3 %collective-permute-start.7 = (bf16[256,384]{1,0:T(8,128)(2,1)}, bf16[256,384]{1,0:T(8,128)(2,1)S(1)}, u32[]{:S(2)}, u32[]{:S(2)}) collective-permute-start(bf16[256,384]{1,0:T(8,128)(2,1)} %get-tuple-element.129.low_ref.low2_ref), channel_id=1, source_target_pairs={{0,2},{2,0},{1,3},{3,1},{4,6},{6,4},{5,7},{7,5},{8,10},{10,8},{9,1... | collective-permute-start | bytes 589832 | tf_op jit(solution)/shard_map/ppermute | solution.py:885
  153.3 116.9 %reduce-scatter.2.cloned.1.call-start = ((), (), s32[]{:S(2)}) async-start(), calls=%async_computation.2 | async-start | bytes 1966080 | tf_op jit(solution)/shard_map/reduce_scatter | solution.py:1131
  159.0 59.6 %collective-permute-start.14 = (bf16[384,3072]{1,0:T(8,128)(2,1)}, bf16[384,3072]{1,0:T(8,128)(2,1)}, u32[]{:S(2)}, u32[]{:S(2)}) collective-permute-start(bf16[384,3072]{1,0:T(8,128)(2,1)} %get-tuple-element.157), channel_id=1, source_target_pairs={{0,1},{1,0},{2,3},{3,2},{4,5},{5,4},{6,7},{7,6},{8,9},{9,8},{10,11... | collective-permute-start | bytes 7077896 | tf_op jit(solution)/shard_map/ppermute | solution.py:1087
  166.1 48.2 %collective-permute-start.15 = (bf16[1024,768]{1,0:T(8,128)(2,1)}, bf16[1024,768]{1,0:T(8,128)(2,1)S(1)}, u32[]{:S(2)}, u32[]{:S(2)}) collective-permute-start(bf16[1024,768]{1,0:T(8,128)(2,1)} %get-tuple-element.159), channel_id=1, source_target_pairs={{0,4},{4,0},{1,5},{5,1},{2,6},{6,2},{3,7},{7,3},{8,12},{12,8},{9,1... | collective-permute-start | bytes 4718600 | tf_op jit(solution)/shard_map/ppermute | solution.py:908
  218.5 188.7 %all-gather.10.cloned.1.call-start = ((), (), s32[]{:S(2)}) async-start(), calls=%async_computation.4 | async-start | bytes 7520256 | tf_op jit(solution)/shard_map/all_gather | solution.py:1179
  221.4 27.3 %collective-permute-start.16 = (bf16[192,3072]{1,0:T(8,128)(2,1)}, bf16[192,3072]{1,0:T(8,128)(2,1)}, u32[]{:S(2)}, u32[]{:S(2)}) collective-permute-start(bf16[192,3072]{1,0:T(8,128)(2,1)} %add_convert_fusion.2), channel_id=1, source_target_pairs={{0,4},{4,0},{1,5},{5,1},{2,6},{6,2},{3,7},{7,3},{8,12},{12,8},{9,1... | collective-permute-start | bytes 3538952 | tf_op jit(solution)/shard_map/ppermute | solution.py:908
  223.9 29.2 %collective-permute-start.18 = (bf16[384,1536]{1,0:T(8,128)(2,1)}, bf16[384,1536]{1,0:T(8,128)(2,1)}, u32[]{:S(2)}, u32[]{:S(2)}) collective-permute-start(bf16[384,1536]{1,0:T(8,128)(2,1)} %get-tuple-element.183), channel_id=1, source_target_pairs={{0,1},{1,0},{2,3},{3,2},{4,5},{5,4},{6,7},{7,6},{8,9},{9,8},{10,11... | collective-permute-start | bytes 3538952 | tf_op jit(solution)/shard_map/ppermute | solution.py:1103
  246.8 19.0 %collective-permute-start.19 = (bf16[384,896]{1,0:T(8,128)(2,1)}, bf16[384,896]{1,0:T(8,128)(2,1)}, u32[]{:S(2)}, u32[]{:S(2)}) collective-permute-start(bf16[384,896]{1,0:T(8,128)(2,1)} %get-tuple-element.179), channel_id=1, source_target_pairs={{0,1},{1,0},{2,3},{3,2},{4,5},{5,4},{6,7},{7,6},{8,9},{9,8},{10,11... | collective-permute-start | bytes 2064392 | tf_op jit(solution)/shard_map/ppermute | solution.py:1103
  251.2 22.6 %collective-permute-start.17 = (bf16[96,3072]{1,0:T(8,128)(2,1)}, bf16[96,3072]{1,0:T(8,128)(2,1)}, u32[]{:S(2)}, u32[]{:S(2)}) collective-permute-start(bf16[96,3072]{1,0:T(8,128)(2,1)} %add_convert_fusion.4), channel_id=1, source_target_pairs={{0,8},{8,0},{16,24},{24,16},{1,9},{9,1},{17,25},{25,17},{2,10},{10... | collective-permute-start | bytes 1769480 | tf_op jit(solution)/shard_map/ppermute | solution.py:908
  269.7 20.8 %collective-permute-start.23 = (bf16[192,2432]{1,0:T(8,128)(2,1)}, bf16[192,2432]{1,0:T(8,128)(2,1)S(1)}, u32[]{:S(2)}, u32[]{:S(2)}) collective-permute-start(bf16[192,2432]{1,0:T(8,128)(2,1)} %fusion.2), channel_id=1, source_target_pairs={{0,4},{4,0},{1,5},{5,1},{2,6},{6,2},{3,7},{7,3},{8,12},{12,8},{9,1... | collective-permute-start | bytes 2801672 | tf_op jit(solution)/shard_map/ppermute | solution.py:908
  276.1 7.5 %collective-permute-start.21 = (f32[128,768]{1,0:T(8,128)}, f32[128,768]{1,0:T(8,128)}, u32[]{:S(2)}, u32[]{:S(2)}) collective-permute-start(f32[128,768]{1,0:T(8,128)} %get-tuple-element.196), channel_id=1, source_target_pairs={{0,2},{2,0},{1,3},{3,1},{4,6},{6,4},{5,7},{7,5},{8,10},{10,8},{9,1... | collective-permute-start | bytes 1179656 | tf_op jit(solution)/shard_map/ppermute | solution.py:885
  276.6 15.6 %collective-permute-start.22 = (bf16[384,768]{1,0:T(8,128)(2,1)}, bf16[384,768]{1,0:T(8,128)(2,1)}, u32[]{:S(2)}, u32[]{:S(2)}) collective-permute-start(bf16[384,768]{1,0:T(8,128)(2,1)} %get-tuple-element.190), channel_id=1, source_target_pairs={{0,1},{1,0},{2,3},{3,2},{4,5},{5,4},{6,7},{7,6},{8,9},{9,8},{10,11... | collective-permute-start | bytes 1769480 | tf_op jit(solution)/shard_map/ppermute | solution.py:1103
  277.8 17.0 %collective-permute-start.26 = (bf16[48,3072]{1,0:T(8,128)(2,1)}, bf16[48,3072]{1,0:T(8,128)(2,1)S(1)}, u32[]{:S(2)}, u32[]{:S(2)}) collective-permute-start(bf16[48,3072]{1,0:T(8,128)(2,1)} %add_convert_fusion.8), channel_id=1, source_target_pairs={{0,16},{8,24},{16,0},{24,8},{1,17},{9,25},{17,1},{25,9},{2,18},{10... | collective-permute-start | bytes 884744 | tf_op jit(solution)/shard_map/ppermute | solution.py:908
  290.8 13.1 %collective-permute-start.25 = (bf16[96,2432]{1,0:T(8,128)(2,1)S(1)}, bf16[96,2432]{1,0:T(8,128)(2,1)S(1)}, u32[]{:S(2)}, u32[]{:S(2)}) collective-permute-start(bf16[96,2432]{1,0:T(8,128)(2,1)S(1)} %add_convert_fusion.5), channel_id=1, source_target_pairs={{0,8},{8,0},{16,24},{24,16},{1,9},{9,1},{17,25},{25,17},{2,10},{10... | collective-permute-start | bytes 1400840 | tf_op jit(solution)/shard_map/ppermute | solution.py:908
  293.2 12.5 %collective-permute-start.24 = (bf16[192,768]{1,0:T(8,128)(2,1)S(1)}, bf16[192,768]{1,0:T(8,128)(2,1)S(1)}, u32[]{:S(2)}, u32[]{:S(2)}) collective-permute-start(bf16[192,768]{1,0:T(8,128)(2,1)S(1)} %add_convert_fusion.7), channel_id=1, source_target_pairs={{0,4},{4,0},{1,5},{5,1},{2,6},{6,2},{3,7},{7,3},{8,12},{12,8},{9,1... | collective-permute-start | bytes 884744 | tf_op jit(solution)/shard_map/ppermute | solution.py:908
  304.1 13.1 %collective-permute-start.28 = (bf16[48,2432]{1,0:T(8,128)(2,1)S(1)}, bf16[48,2432]{1,0:T(8,128)(2,1)S(1)}, u32[]{:S(2)}, u32[]{:S(2)}) collective-permute-start(bf16[48,2432]{1,0:T(8,128)(2,1)S(1)} %add_convert_fusion.10), channel_id=1, source_target_pairs={{0,16},{8,24},{16,0},{24,8},{1,17},{9,25},{17,1},{25,9},{2,18},{10... | collective-permute-start | bytes 700424 | tf_op jit(solution)/shard_map/ppermute | solution.py:908
  318.2 5.2 %collective-permute-start.27 = (bf16[96,768]{1,0:T(8,128)(2,1)S(1)}, bf16[96,768]{1,0:T(8,128)(2,1)S(1)}, u32[]{:S(2)}, u32[]{:S(2)}) collective-permute-start(bf16[96,768]{1,0:T(8,128)(2,1)S(1)} %add_convert_fusion.11), channel_id=1, source_target_pairs={{0,8},{8,0},{16,24},{24,16},{1,9},{9,1},{17,25},{25,17},{2,10},{10... | collective-permute-start | bytes 442376 | tf_op jit(solution)/shard_map/ppermute | solution.py:908
  324.5 6.2 %collective-permute-start.29 = (bf16[48,768]{1,0:T(8,128)(2,1)S(1)}, bf16[48,768]{1,0:T(8,128)(2,1)S(1)}, u32[]{:S(2)}, u32[]{:S(2)}) collective-permute-start(bf16[48,768]{1,0:T(8,128)(2,1)S(1)} %add_convert_fusion.13), channel_id=1, source_target_pairs={{0,16},{8,24},{16,0},{24,8},{1,17},{9,25},{17,1},{25,9},{2,18},{10... | collective-permute-start | bytes 221192 | tf_op jit(solution)/shard_map/ppermute | solution.py:908
  331.6 17.1 %collective-permute-start.30 = (bf16[48,1664]{1,0:T(8,128)(2,1)S(1)}, bf16[48,1664]{1,0:T(8,128)(2,1)S(1)}, u32[]{:S(2)}, u32[]{:S(2)}) collective-permute-start(bf16[48,1664]{1,0:T(8,128)(2,1)S(1)} %pad_maximum_fusion.5), channel_id=1, source_target_pairs={{0,16},{8,24},{16,0},{24,8},{1,17},{9,25},{17,1},{25,9},{2,18},{10... | collective-permute-start | bytes 479240 | tf_op jit(solution)/shard_map/ppermute | solution.py:908
  348.8 8.5 %collective-permute-start.31 = (bf16[96,1664]{1,0:T(8,128)(2,1)S(1)}, bf16[96,1664]{1,0:T(8,128)(2,1)S(1)}, u32[]{:S(2)}, u32[]{:S(2)}) collective-permute-start(bf16[96,1664]{1,0:T(8,128)(2,1)S(1)} %pad_maximum_fusion.4), channel_id=1, source_target_pairs={{0,8},{8,0},{16,24},{24,16},{1,9},{9,1},{17,25},{25,17},{2,10},{10... | collective-permute-start | bytes 958472 | tf_op jit(solution)/shard_map/ppermute | solution.py:908
  357.4 30.3 %collective-permute-start.32 = (bf16[192,1664]{1,0:T(8,128)(2,1)S(1)}, bf16[192,1664]{1,0:T(8,128)(2,1)S(1)}, u32[]{:S(2)}, u32[]{:S(2)}) collective-permute-start(bf16[192,1664]{1,0:T(8,128)(2,1)S(1)} %pad_maximum_fusion.1), channel_id=1, source_target_pairs={{0,4},{4,0},{1,5},{5,1},{2,6},{6,2},{3,7},{7,3},{8,12},{12,8},{9,1... | collective-permute-start | bytes 1916936 | tf_op jit(solution)/shard_map/ppermute | solution.py:908
  (38 other events, 325.4 us)
Sparse Core Ops, SparseCore 0:
  10.9 64.5 all-gather.5
  153.4 65.9 all-gather.7
  221.7 34.3 reduce-scatter.1
  318.4 88.7 all-gather.9
where the time goes:
time: 428 us; the launch traced here: 423 us
  waiting for transfers between devices  192 us (45%)
  Pallas kernels  128 us (30%)
  starting transfers between devices  42.5 us (10%)
  other arithmetic  28.3 us (7%)
  local copies, waits for them, and re-layouts  15.2 us (4%)
  between operations  14.7 us (3%)
    pallas_call x14, Pallas kernels, call(): pl.pallas_call(kernel, out_shape=[jax.ShapeDtypeStruct(s, d) for s, d in...  120 us
    ppermute x13, waiting for transfers between devices, swap_bit(): lax.ppermute(value, axis, [(i, i ^ 1 << bit) for i in range(lax.axis_size...  113 us
    ppermute x6, waiting for transfers between devices, gather_fsdp(): return [own, lax.ppermute(own, 'fsdp', [(0, 1), (1, 0)])]  43 us
    ppermute x13, starting transfers between devices, swap_bit(): lax.ppermute(value, axis, [(i, i ^ 1 << bit) for i in range(lax.axis_size...  20.8 us
    ppermute x3, waiting for transfers between devices, over_fsdp(): return [parts[0], lax.ppermute(parts[1], 'fsdp', [(0, 1), (1, 0)])]  13.1 us
    convert_element_type x8, other arithmetic, parted(): return (half(side), total(half(1 - side)).astype(BF16))  10.9 us
    unnamed x73, local copies, waits for them, and re-layouts  9.46 us
    ppermute x6, starting transfers between devices, gather_fsdp(): return [own, lax.ppermute(own, 'fsdp', [(0, 1), (1, 0)])]  9.3 us
  transfers between devices with their start and end apart: 38, of which 22 were waited for; matrix products, arithmetic and copies ran while one was open for 8% of the time, Pallas kernels for 22%

commit v1 on v0

--- a/solution.py
+++ b/solution.py
@@ -1145,12 +1145,12 @@
     first = scatter(first_keep + [after(first_got, fourth_sent)], y_steps[1:])
     first_keep, first_sent = parted(first, *z_near)
     first_got = swap_bit(first_sent, *z_near)
-    second, fourth = after((second, fourth), first_sent)
-    second = jnp.concatenate([total(second), total(fourth)], axis=1).astype(BF16)
-    second_keep, second_sent = parted([second], *y_steps[0])
+    second_keep, second_sent = parted(after(second, first_sent), *y_steps[0])
     second_got = swap_bit(second_sent, *y_steps[0])
+    fourth_keep, fourth_sent = parted(after(fourth, second_sent), *y_steps[0])
+    fourth_got = swap_bit(fourth_sent, *y_steps[0])
     enc_keep, enc_send, *third = call(
-        functools.partial(encoder_grads_kernel, n_fsdp), (at,), (after(dkv_cross, second_sent), e_chip, w_cross),
+        functools.partial(encoder_grads_kernel, n_fsdp), (at,), (after(dkv_cross, fourth_sent), e_chip, w_cross),
         [half_rows, half_rows, *given(2 * HALF)],
         [((ROWS, 2 * HALF), BF16), wide, ((width, 2 * HALF), BF16)], 8 * ROWS * width * HALF,
     )
@@ -1158,15 +1158,19 @@
     third = over_fsdp(third)
     first_keep, first_sent = parted(first_keep + [after(first_got, third_sent)], *z_far)
     first_got = swap_bit(first_sent, *z_far)
+
+    second_got, fourth_got = after((second_got, fourth_got), first_sent)
+    second = total(scatter(second_keep + [second_got], y_steps[1:]))
+    fourth = total(scatter(fourth_keep + [fourth_got], y_steps[1:]))
+    second = jnp.concatenate([second, fourth], axis=1).astype(BF16)
+    second_keep, second_sent = parted([second], *z_near)
+    second_got = swap_bit(second_sent, *z_near)
     (grad_tokens,) = call(
-        token_grads_kernel, (at,), (e_keep, swap_core(after(e_send, first_sent)), tokens, gain_self, grad_mid),
+        token_grads_kernel, (at,), (e_keep, swap_core(after(e_send, second_sent)), tokens, gain_self, grad_mid),
         [half_rows], [], 10 * rows * width,
     )
-    enc_grad = enc_keep + swap_core(after(enc_send, first_sent))
-
-    second = scatter(second_keep + [after(second_got, grad_tokens, enc_grad)], y_steps[1:])
-    second_keep, second_sent = parted(second, *z_near)
-    second_got = swap_bit(second_sent, *z_near)
+    enc_grad = enc_keep + swap_core(after(enc_send, second_sent))
+    second_got = after(second_got, grad_tokens, enc_grad)
     late_keep, late_sent = parted(after(third, second_sent), *y_steps[0])
     late_got = swap_bit(late_sent, *y_steps[0])
     first = total(first_keep + [after(first_got, late_sent)]).astype(BF16)

time: 428 us -> 415 us (0.970)
  starting transfers between devices: 42.5 us -> 23.4 us
  Pallas kernels: 128 us -> 136 us
    ppermute x13 -> x14, starting transfers between devices: 20.8 us -> 6.35 us  [swap_bit(): lax.ppermute(value, axis, [(i, i ^ 1 << bit) for i in range(lax.axis_size...]
    pallas_call x14, Pallas kernels: 120 us -> 128 us  [call(): pl.pallas_call(kernel, out_shape=[jax.ShapeDtypeStruct(s, d) for s, d in...]
    ppermute x1, waiting for transfers between devices: 0.01 us -> 6.61 us  [on_device(): first_other = lax.ppermute(first[1], 'fsdp', [(0, 1), (1, 0)])]
    ppermute x1, starting transfers between devices: 7.08 us -> 1.75 us  [on_device(): first_other = lax.ppermute(first[1], 'fsdp', [(0, 1), (1, 0)])]
    all_gather x1, waiting for transfers between devices: 9.19 us -> 4.32 us  [on_device(): lax.all_gather(jnp.concatenate([first, second[:, :4 * HALF]], axis=1), GR...]
    ppermute x13 -> x14, waiting for transfers between devices: 113 us -> 109 us  [swap_bit(): lax.ppermute(value, axis, [(i, i ^ 1 << bit) for i in range(lax.axis_size...]
    convert_element_type x8 -> x9, other arithmetic: 10.9 us -> 11.8 us  [parted(): return (half(side), total(half(1 - side)).astype(BF16))]
    unnamed x73 -> x79, local copies, waits for them, and re-layouts: 9.46 us -> 9.59 us
  transfers between devices with their start and end apart: 38 -> 39, of which waited for: 22 -> 24; matrix products, arithmetic and copies ran while one was open for 8% -> 8% of each run, Pallas kernels for 22% -> 24%
where the time goes in v1:
time: 415 us; the launch traced here: 409 us
  waiting for transfers between devices  190 us (46%)
  Pallas kernels  136 us (33%)
  other arithmetic  26.9 us (6%)
  starting transfers between devices  23.4 us (6%)
  local copies, waits for them, and re-layouts  15.3 us (4%)
  between operations  14.8 us (4%)
    pallas_call x14, Pallas kernels, call(): pl.pallas_call(kernel, out_shape=[jax.ShapeDtypeStruct(s, d) for s, d in...  128 us
    ppermute x14, waiting for transfers between devices, swap_bit(): lax.ppermute(value, axis, [(i, i ^ 1 << bit) for i in range(lax.axis_size...  109 us
    ppermute x6, waiting for transfers between devices, gather_fsdp(): return [own, lax.ppermute(own, 'fsdp', [(0, 1), (1, 0)])]  40.1 us
    ppermute x3, waiting for transfers between devices, over_fsdp(): return [parts[0], lax.ppermute(parts[1], 'fsdp', [(0, 1), (1, 0)])]  16.3 us
    convert_element_type x9, other arithmetic, parted(): return (half(side), total(half(1 - side)).astype(BF16))  11.8 us
    unnamed x79, local copies, waits for them, and re-layouts  9.59 us
    ppermute x6, starting transfers between devices, gather_fsdp(): return [own, lax.ppermute(own, 'fsdp', [(0, 1), (1, 0)])]  9.3 us
  transfers between devices with their start and end apart: 39, of which 24 were waited for; matrix products, arithmetic and copies ran while one was open for 8% of the time, Pallas kernels for 24%

profile of v1, /device:TPU:0, one launch (start us, length us, event | category | flops | bytes accessed | tf_op | source)
XLA Modules:
  0.0 408.9 jit_solution(12415288067451218531)
XLA Ops:
  9.2 5.3 %shard_map.362 = (bf16[384,768]{1,0:T(8,128)(2,1)}, bf16[384,1152]{1,0:T(8,128)(2,1)}, bf16[384,1536]{1,0:T(8,128)(2,1)}, bf16[768,768]{1,0:T(8,128)(2,1)}) custom-call(s32[1]{0:T(128)} %bitcast.1.core_ref, f32[384,768]{1,0:T(8,128)} %refs_0_.3, f32[384,768]{1,0:T(8,128)} %refs_1_.3, f32[384,768]{1,0:T(8,128)} %refs_2_.3, f32[384,768]{1,0:T(8,128)} %refs_3_.1, ...), custom_call_target="tpu_custom_call" | custom-call | tf_op jit(solution)/shard_map/pallas_call | solution.py:867
  14.4 2.9 collective-permute-start.6
  22.4 15.7 %collective-permute-done.6.refs_5_ = bf16[384,1152]{1,0:T(8,128)(2,1)S(1)} collective-permute-done((bf16[384,1152]{1,0:T(8,128)(2,1)}, bf16[384,1152]{1,0:T(8,128)(2,1)S(1)}, u32[]{:S(2)}, u32[]{:S(2)}) %collective-permute-start.6) | collective-permute-done | bytes 884768 | tf_op jit(solution)/shard_map/ppermute | solution.py:892
  41.0 9.8 %collective-permute-done = bf16[1,1344]{1,0:T(2,128)(2,1)S(1)} collective-permute-done((bf16[1,1344]{1,0:T(2,128)(2,1)S(1)}, bf16[1,1344]{1,0:T(2,128)(2,1)S(1)}, u32[]{:S(2)}, u32[]{:S(2)}) %collective-permute-start) | collective-permute-done | bytes 2720 | tf_op jit(solution)/shard_map/ppermute | solution.py:892
  58.4 3.8 shard_map.359.tiles
  62.8 7.1 %collective-permute-done.1.refs_1_ = bf16[384,1152]{1,0:T(8,128)(2,1)} collective-permute-done((bf16[384,1152]{1,0:T(8,128)(2,1)}, bf16[384,1152]{1,0:T(8,128)(2,1)}, u32[]{:S(2)}, u32[]{:S(2)}) %collective-permute-start.1) | collective-permute-done | bytes 884768 | tf_op jit(solution)/shard_map/ppermute | solution.py:892
  69.9 5.6 %all-gather.6.cloned.1.call-done.xe_ref = bf16[2048,1536]{1,0:T(8,128)(2,1)} async-done(((bf16[128,1536]{1,0:T(8,128)(2,1)}), bf16[2048,1536]{1,0:T(8,128)(2,1)}) %all-gather.6.cloned.1.call-update) | async-done | bytes 6291472 | tf_op jit(solution)/shard_map/all_gather | solution.py:900
  75.5 14.3 %shard_map.361 = (bf16[9,2048,128]{2,1,0:T(8,128)(2,1)}, bf16[768,1152]{1,0:T(8,128)(2,1)}, f32[256,384]{1,0:T(8,128)}, bf16[256,384]{1,0:T(8,128)(2,1)}, f32[256,128]{1,0:T(8,128)}) custom-call(s32[4]{0:T(128)} %pad_add_fusion.at_ref, s32[1,6]{1,0:T(1,128)} %len_ref.9, bf16[2048,1536]{1,0:T(8,128)(2,1)} %all-gather.6.cloned.1.call-done.xe_ref, ...), custom_call_target="tpu_custom_call" | custom-call | flops 1 | bytes 1 | tf_op jit(solution)/shard_map/pallas_call | solution.py:847
  92.1 19.1 %shard_map.363 = (f32[256,768]{1,0:T(8,128)}, bf16[256,768]{1,0:T(8,128)(2,1)}, bf16[256,384]{1,0:T(8,128)(2,1)}, bf16[6,2048,128]{2,1,0:T(8,128)(2,1)}, f32[256...) custom-call(s32[4]{0:T(128)} %pad_add_fusion.at_ref, ...), custom_call_target="tpu_custom_call" | custom-call | flops 1 | bytes 1 | tf_op jit(solution)/shard_map/pallas_call | solution.py:847
  112.1 7.5 %collective-permute-done.10.refs_3_ = bf16[768,768]{1,0:T(8,128)(2,1)} collective-permute-done((bf16[768,768]{1,0:T(8,128)(2,1)S(1)}, bf16[768,768]{1,0:T(8,128)(2,1)}, u32[]{:S(2)}, u32[]{:S(2)}) %collective-permute-start.10) | collective-permute-done | bytes 1179680 | tf_op jit(solution)/shard_map/ppermute | solution.py:892
  120.3 8.7 %shard_map.364 = (f32[256,768]{1,0:T(8,128)}, bf16[256,768]{1,0:T(8,128)(2,1)}, bf16[256,1536]{1,0:T(8,128)(2,1)}, bf16[256,1536]{1,0:T(8,128)(2,1)}, bf16[256,7...) custom-call(s32[4]{0:T(128)} %pad_add_fusion.at_ref, ...), custom_call_target="tpu_custom_call" | custom-call | flops 1 | bytes 1 | tf_op jit(solution)/shard_map/pallas_call | solution.py:847
  132.4 18.7 %shard_map.365 = (f32[256,768]{1,0:T(8,128)}, bf16[256,768]{1,0:T(8,128)(2,1)}, f32[1,768]{1,0:T(1,128)}, bf16[256,384]{1,0:T(8,128)(2,1)}, bf16[1024,768]{1,0:T...) custom-call(s32[4]{0:T(128)} %pad_add_fusion.at_ref, s32[1,6]{1,0:T(1,128)} %len_ref.9, s32[1,6]{1,0:T(1,128)} %enc_ref.3, ...), custom_call_target="tpu_custom_call" | custom-call | flops 1 | bytes 1 | tf_op jit(solution)/shard_map/pallas_call | solution.py:847
  154.5 4.2 %shard_map.366 = (f32[256,768]{1,0:T(8,128)}, bf16[256,768]{1,0:T(8,128)(2,1)}, f32[1,768]{1,0:T(1,128)}, bf16[256,384]{1,0:T(8,128)(2,1)}, bf16[144,768]{1,0:T(8,128)(2,1)}) custom-call(s32[4]{0:T(128)} %pad_add_fusion.at_ref, f32[256,768]{1,0:T(8,128)} %get-tuple-element.148.e_ref, f32[256,768]{1,0:T(8,128)} %copy-done.11, ...), custom_call_target="tpu_custom_call" | custom-call | flops 1 | bytes 1 | tf_op jit(solution)/shard_map/pallas_call | solution.py:847
  158.8 5.7 %shard_map.367 = (bf16[384,3072]{1,0:T(8,128)(2,1)}, bf16[384,3072]{1,0:T(8,128)(2,1)}) custom-call(s32[4]{0:T(128)} %pad_add_fusion.at_ref, bf16[256,1536]{1,0:T(8,128)(2,1)} %get-tuple-element.154.hid_ref, bf16[256,768]{1,0:T(8,128)(2,1)} %get-tuple-element.142.cot_ref, bf16[256,768]{1,0:T(8,128)(2,1)} %get-tuple-element.155.in_ref, ...), custom_call_target="tpu_custom_call" | custom-call | flops 1 | bytes 1 | tf_op jit(solution)/shard_map/pallas_call | solution.py:847
  168.4 9.4 %shard_map.368 = (bf16[256,384]{1,0:T(8,128)(2,1)}, f32[8,512]{1,0:T(8,128)}) custom-call(s32[4]{0:T(128)} %pad_add_fusion.at_ref, s32[1,6]{1,0:T(1,128)} %len_ref.9, bf16[2,3,6,256,256]{4,3,2,1,0:T(8,128)(2,1)} %shard_map.359.tiles, bf16[9,2048,128]{2,1,0:T(8,128)(2,1)} %get-tuple-element.139.qkv_ref, bf16[256,384]{1,0:T(8,128)(2,1)} %get-tuple-element.167.go_ref, ...), custom_call_target="tpu_custom_call" | custom-call | flops 1 | bytes 1 | tf_op jit(solution)/shard_map/pallas_call | solution.py:847
  177.8 4.4 %shard_map.369 = (bf16[384,1536]{1,0:T(8,128)(2,1)}, bf16[384,1536]{1,0:T(8,128)(2,1)}) custom-call(s32[4]{0:T(128)} %pad_add_fusion.at_ref, bf16[256,384]{1,0:T(8,128)(2,1)} %get-tuple-element.131.low_ref.low2_ref, bf16[256,384]{1,0:T(8,128)(2,1)} %copy-done.12, bf16[256,768]{1,0:T(8,128)(2,1)} %get-tuple-element.162.b2_ref, ...), custom_call_target="tpu_custom_call" | custom-call | flops 1 | bytes 1 | tf_op jit(solution)/shard_map/pallas_call | solution.py:847
  182.2 25.0 %collective-permute-done.15 = bf16[1024,768]{1,0:T(8,128)(2,1)S(1)} collective-permute-done((bf16[1024,768]{1,0:T(8,128)(2,1)S(1)}, bf16[1024,768]{1,0:T(8,128)(2,1)S(1)}, u32[]{:S(2)}, u32[]{:S(2)}) %collective-permute-start.15) | collective-permute-done | bytes 1572896 | tf_op jit(solution)/shard_map/ppermute | solution.py:908
  208.4 3.1 add_convert_fusion
  211.6 6.6 %collective-permute-done.14 = bf16[384,3072]{1,0:T(8,128)(2,1)} collective-permute-done((bf16[384,3072]{1,0:T(8,128)(2,1)}, bf16[384,3072]{1,0:T(8,128)(2,1)}, u32[]{:S(2)}, u32[]{:S(2)}) %collective-permute-start.14) | collective-permute-done | bytes 2359328 | tf_op jit(solution)/shard_map/ppermute | solution.py:1087
  227.3 20.7 %shard_map.370 = (f32[128,768]{1,0:T(8,128)}, f32[128,768]{1,0:T(8,128)}, bf16[384,896]{1,0:T(8,128)(2,1)}, bf16[384,896]{1,0:T(8,128)(2,1)}) custom-call(s32[4]{0:T(128)} %pad_add_fusion.at_ref, s32[1,6]{1,0:T(1,128)} %len_ref.9, bf16[2,3,6,256,256]{4,3,2,1,0:T(8,128)(2,1)} %shard_map.359.tiles, bf16[9,2048,128]{2,1,0:T(8,128)(2,1)} %get-tuple-element.139.qkv_ref, ...), custom_call_target="tpu_custom_call" | custom-call | flops 1 | bytes 1 | tf_op jit(solution)/shard_map/pallas_call | solution.py:847
  255.0 10.1 %collective-permute-done.19 = bf16[384,896]{1,0:T(8,128)(2,1)} collective-permute-done((bf16[384,896]{1,0:T(8,128)(2,1)}, bf16[384,896]{1,0:T(8,128)(2,1)}, u32[]{:S(2)}, u32[]{:S(2)}) %collective-permute-start.19) | collective-permute-done | bytes 688160 | tf_op jit(solution)/shard_map/ppermute | solution.py:1103
  267.6 3.7 shard_map.371
  279.5 5.2 %collective-permute-done.24 = bf16[384,768]{1,0:T(8,128)(2,1)S(1)} collective-permute-done((bf16[384,768]{1,0:T(8,128)(2,1)}, bf16[384,768]{1,0:T(8,128)(2,1)S(1)}, u32[]{:S(2)}, u32[]{:S(2)}) %collective-permute-start.24) | collective-permute-done | bytes 589856 | tf_op jit(solution)/shard_map/ppermute | solution.py:1103
  294.1 12.4 %collective-permute-done.29 = bf16[48,2432]{1,0:T(8,128)(2,1)S(1)} collective-permute-done((bf16[48,2432]{1,0:T(8,128)(2,1)S(1)}, bf16[48,2432]{1,0:T(8,128)(2,1)S(1)}, u32[]{:S(2)}, u32[]{:S(2)}) %collective-permute-start.29) | collective-permute-done | bytes 233504 | tf_op jit(solution)/shard_map/ppermute | solution.py:908
  307.5 5.8 %collective-permute-done.28 = bf16[96,768]{1,0:T(8,128)(2,1)S(1)} collective-permute-done((bf16[96,768]{1,0:T(8,128)(2,1)S(1)}, bf16[96,768]{1,0:T(8,128)(2,1)S(1)}, u32[]{:S(2)}, u32[]{:S(2)}) %collective-permute-start.28) | collective-permute-done | bytes 147488 | tf_op jit(solution)/shard_map/ppermute | solution.py:908
  314.3 12.3 %collective-permute-done.30 = bf16[48,768]{1,0:T(8,128)(2,1)S(1)} collective-permute-done((bf16[48,768]{1,0:T(8,128)(2,1)S(1)}, bf16[48,768]{1,0:T(8,128)(2,1)S(1)}, u32[]{:S(2)}, u32[]{:S(2)}) %collective-permute-start.30) | collective-permute-done | bytes 73760 | tf_op jit(solution)/shard_map/ppermute | solution.py:908
  327.7 13.0 %collective-permute-done.31 = bf16[48,1664]{1,0:T(8,128)(2,1)S(1)} collective-permute-done((bf16[48,1664]{1,0:T(8,128)(2,1)S(1)}, bf16[48,1664]{1,0:T(8,128)(2,1)S(1)}, u32[]{:S(2)}, u32[]{:S(2)}) %collective-permute-start.31) | collective-permute-done | bytes 159776 | tf_op jit(solution)/shard_map/ppermute | solution.py:908
  340.9 21.0 %collective-permute-done.32 = bf16[96,1664]{1,0:T(8,128)(2,1)S(1)} collective-permute-done((bf16[96,1664]{1,0:T(8,128)(2,1)S(1)}, bf16[96,1664]{1,0:T(8,128)(2,1)S(1)}, u32[]{:S(2)}, u32[]{:S(2)}) %collective-permute-start.32) | collective-permute-done | bytes 319520 | tf_op jit(solution)/shard_map/ppermute | solution.py:908
  362.3 16.6 %collective-permute-done.33 = bf16[192,1664]{1,0:T(8,128)(2,1)S(1)} collective-permute-done((bf16[192,1664]{1,0:T(8,128)(2,1)S(1)}, bf16[192,1664]{1,0:T(8,128)(2,1)S(1)}, u32[]{:S(2)}, u32[]{:S(2)}) %collective-permute-start.33) | collective-permute-done | bytes 639008 | tf_op jit(solution)/shard_map/ppermute | solution.py:908
  384.3 5.0 %shard_map.373 = (f32[384,768]{1,0:T(8,128)}, f32[384,768]{1,0:T(8,128)}, f32[384,768]{1,0:T(8,128)}, f32[384,768]{1,0:T(8,128)}, f32[384]{0:T(512)}, /*index=5*/f32[384]{0:T(512)}, f32[384]{0:T(512)}, f32[16,12]{1,0:T(8,128)}) custom-call(s32[4]{0:T(128)} %pad_add_fusion.at_ref, s32[1]{0:T(128)} %dynamic_slice.198.place_ref, bf16[384,1664]{1,0:T(8,128)(2,1)} %copy-done, ...), custom_call_target="tpu_custom_call" | custom-call | flops 1 | bytes 1 | tf_op jit(solution)/shard_map/pallas_call | solution.py:847
  389.3 4.3 %all-gather.10.cloned.1.call-done = bf16[768,4608]{1,0:T(8,128)(2,1)} async-done(((bf16[48,4608]{1,0:T(8,128)(2,1)}), bf16[768,4608]{1,0:T(8,128)(2,1)}) %all-gather.10.cloned.1.call-update) | async-done | bytes 7077904 | tf_op jit(solution)/shard_map/all_gather | solution.py:1183
  393.6 8.4 %shard_map.374 = (f32[1536,768]{1,0:T(8,128)}, f32[384,3072]{1,0:T(8,128)}, f32[384,768]{1,0:T(8,128)}, f32[384,768]{1,0:T(8,128)}, f32[384,768]{1,0:T(8,128)}, /*index=5*/f32[384,768]{1,0:T(8,128)}) custom-call(bf16[16,48,4608]{2,1,0:T(8,128)(2,1)} %bitcast.45), custom_call_target="tpu_custom_call" | custom-call | flops 1 | bytes 1 | tf_op jit(solution)/shard_map/pallas_call | solution.py:847
  (196 shorter events, 78.8 us)
Async XLA Ops:
  7.2 68.3 %all-gather.6.cloned.1.call-start = ((), (), s32[]{:S(2)}) async-start(), calls=%async_computation.1 | async-start | bytes 6684672 | tf_op jit(solution)/shard_map/all_gather | solution.py:900
  9.1 218.2 %all-gather.8.cloned.1.call-start = ((), (), s32[]{:S(2)}) async-start(), calls=%async_computation.3 | async-start | bytes 3760128 | tf_op jit(solution)/shard_map/all_gather | solution.py:1089
  14.4 23.6 %collective-permute-start.6 = (bf16[384,1152]{1,0:T(8,128)(2,1)}, bf16[384,1152]{1,0:T(8,128)(2,1)S(1)}, u32[]{:S(2)}, u32[]{:S(2)}) collective-permute-start(bf16[384,1152]{1,0:T(8,128)(2,1)} %get-tuple-element.129.refs_4_), channel_id=1, source_target_pairs={{0,1},{1,0},{2,3},{3,2},{4,5},{5,4},{6,7},{7,6},{8,9},{9,8},{10,11... | collective-permute-start | bytes 2654216 | tf_op jit(solution)/shard_map/ppermute | solution.py:892
  17.4 39.7 %collective-permute-start.3 = (bf16[384,768]{1,0:T(8,128)(2,1)}, bf16[384,768]{1,0:T(8,128)(2,1)}, u32[]{:S(2)}, u32[]{:S(2)}) collective-permute-start(bf16[384,768]{1,0:T(8,128)(2,1)} %get-tuple-element.128.refs_0_), channel_id=1, source_target_pairs={{0,1},{1,0},{2,3},{3,2},{4,5},{5,4},{6,7},{7,6},{8,9},{9,8},{10,11... | collective-permute-start | bytes 1769480 | tf_op jit(solution)/shard_map/ppermute | solution.py:892
  17.7 33.2 %collective-permute-start = (bf16[1,1344]{1,0:T(2,128)(2,1)S(1)}, bf16[1,1344]{1,0:T(2,128)(2,1)S(1)}, u32[]{:S(2)}, u32[]{:S(2)}) collective-permute-start(bf16[1,1344]{1,0:T(2,128)(2,1)S(1)} %constant_dynamic-update-slice_fusion), channel_id=1, source_target_pairs={{0,1},{1,0},{2,3},{3,2},{4,5},{5,4},{6,7},{7,6},{8,9},{9,8},{10,11... | collective-permute-start | bytes 8072 | tf_op jit(solution)/shard_map/ppermute | solution.py:892
  19.7 70.9 %collective-permute-start.4 = (bf16[384,768]{1,0:T(8,128)(2,1)}, bf16[384,768]{1,0:T(8,128)(2,1)}, u32[]{:S(2)}, u32[]{:S(2)}) collective-permute-start(bf16[384,768]{1,0:T(8,128)(2,1)} %get-tuple-element.128.refs_0_), channel_id=1, source_target_pairs={{0,2},{2,0},{1,3},{3,1},{4,6},{6,4},{5,7},{7,5},{8,10},{10,8},{9,1... | collective-permute-start | bytes 1769480 | tf_op jit(solution)/shard_map/ppermute | solution.py:885
  22.2 47.7 %collective-permute-start.1 = (bf16[384,1152]{1,0:T(8,128)(2,1)}, bf16[384,1152]{1,0:T(8,128)(2,1)}, u32[]{:S(2)}, u32[]{:S(2)}) collective-permute-start(bf16[384,1152]{1,0:T(8,128)(2,1)} %shard_map.360.refs_0_), channel_id=1, source_target_pairs={{0,1},{1,0},{2,3},{3,2},{4,5},{5,4},{6,7},{7,6},{8,9},{9,8},{10,11... | collective-permute-start | bytes 2654216 | tf_op jit(solution)/shard_map/ppermute | solution.py:892
  39.0 73.1 %collective-permute-start.9 = (bf16[384,1536]{1,0:T(8,128)(2,1)S(1)}, bf16[384,1536]{1,0:T(8,128)(2,1)S(1)}, u32[]{:S(2)}, u32[]{:S(2)}) collective-permute-start(bf16[384,1536]{1,0:T(8,128)(2,1)S(1)} %copy-done.6), channel_id=1, source_target_pairs={{0,1},{1,0},{2,3},{3,2},{4,5},{5,4},{6,7},{7,6},{8,9},{9,8},{10,11... | collective-permute-start | bytes 3538952 | tf_op jit(solution)/shard_map/ppermute | solution.py:892
  51.4 68.2 %collective-permute-start.10 = (bf16[768,768]{1,0:T(8,128)(2,1)S(1)}, bf16[768,768]{1,0:T(8,128)(2,1)}, u32[]{:S(2)}, u32[]{:S(2)}) collective-permute-start(bf16[768,768]{1,0:T(8,128)(2,1)S(1)} %copy-done.7), channel_id=1, source_target_pairs={{0,1},{1,0},{2,3},{3,2},{4,5},{5,4},{6,7},{7,6},{8,9},{9,8},{10,11... | collective-permute-start | bytes 3538952 | tf_op jit(solution)/shard_map/ppermute | solution.py:892
  57.1 33.7 %collective-permute-start.5 = (bf16[384,768]{1,0:T(8,128)(2,1)}, bf16[384,768]{1,0:T(8,128)(2,1)}, u32[]{:S(2)}, u32[]{:S(2)}) collective-permute-start(bf16[384,768]{1,0:T(8,128)(2,1)} %collective-permute-done.3.refs_1_), channel_id=1, source_target_pairs={{0,2},{2,0},{1,3},{3,1},{4,6},{6,4},{5,7},{7,5},{8,10},{10,8},{9,1... | collective-permute-start | bytes 1769480 | tf_op jit(solution)/shard_map/ppermute | solution.py:885
  90.6 21.5 %collective-permute-start.8 = (bf16[128,768]{1,0:T(8,128)(2,1)S(1)}, bf16[128,768]{1,0:T(8,128)(2,1)S(1)}, u32[]{:S(2)}, u32[]{:S(2)}) collective-permute-start(bf16[128,768]{1,0:T(8,128)(2,1)S(1)} %copy-done.21), channel_id=1, source_target_pairs={{0,2},{2,0},{1,3},{3,1},{4,6},{6,4},{5,7},{7,5},{8,10},{10,8},{9,1... | collective-permute-start | bytes 589832 | tf_op jit(solution)/shard_map/ppermute | solution.py:885
  158.7 108.9 %reduce-scatter.2.cloned.1.call-start = ((), (), s32[]{:S(2)}) async-start(), calls=%async_computation.2 | async-start | bytes 1966080 | tf_op jit(solution)/shard_map/reduce_scatter | solution.py:1131
  158.8 48.4 %collective-permute-start.15 = (bf16[1024,768]{1,0:T(8,128)(2,1)S(1)}, bf16[1024,768]{1,0:T(8,128)(2,1)S(1)}, u32[]{:S(2)}, u32[]{:S(2)}) collective-permute-start(bf16[1024,768]{1,0:T(8,128)(2,1)S(1)} %copy-done.32), channel_id=1, source_target_pairs={{0,4},{4,0},{1,5},{5,1},{2,6},{6,2},{3,7},{7,3},{8,12},{12,8},{9,1... | collective-permute-start | bytes 4718600 | tf_op jit(solution)/shard_map/ppermute | solution.py:908
  164.6 53.6 %collective-permute-start.14 = (bf16[384,3072]{1,0:T(8,128)(2,1)}, bf16[384,3072]{1,0:T(8,128)(2,1)}, u32[]{:S(2)}, u32[]{:S(2)}) collective-permute-start(bf16[384,3072]{1,0:T(8,128)(2,1)} %get-tuple-element.159), channel_id=1, source_target_pairs={{0,1},{1,0},{2,3},{3,2},{4,5},{5,4},{6,7},{7,6},{8,9},{9,8},{10,11... | collective-permute-start | bytes 7077896 | tf_op jit(solution)/shard_map/ppermute | solution.py:1087
  211.5 182.1 %all-gather.10.cloned.1.call-start = ((), (), s32[]{:S(2)}) async-start(), calls=%async_computation.4 | async-start | bytes 7520256 | tf_op jit(solution)/shard_map/all_gather | solution.py:1183
  221.0 27.5 %collective-permute-start.17 = (bf16[192,3072]{1,0:T(8,128)(2,1)}, bf16[192,3072]{1,0:T(8,128)(2,1)}, u32[]{:S(2)}, u32[]{:S(2)}) collective-permute-start(bf16[192,3072]{1,0:T(8,128)(2,1)} %add_convert_fusion.1), channel_id=1, source_target_pairs={{0,4},{4,0},{1,5},{5,1},{2,6},{6,2},{3,7},{7,3},{8,12},{12,8},{9,1... | collective-permute-start | bytes 3538952 | tf_op jit(solution)/shard_map/ppermute | solution.py:908
  223.4 28.5 %collective-permute-start.16 = (bf16[384,1536]{1,0:T(8,128)(2,1)}, bf16[384,1536]{1,0:T(8,128)(2,1)}, u32[]{:S(2)}, u32[]{:S(2)}) collective-permute-start(bf16[384,1536]{1,0:T(8,128)(2,1)} %get-tuple-element.183), channel_id=1, source_target_pairs={{0,1},{1,0},{2,3},{3,2},{4,5},{5,4},{6,7},{7,6},{8,9},{9,8},{10,11... | collective-permute-start | bytes 3538952 | tf_op jit(solution)/shard_map/ppermute | solution.py:1103
  248.0 17.1 %collective-permute-start.19 = (bf16[384,896]{1,0:T(8,128)(2,1)}, bf16[384,896]{1,0:T(8,128)(2,1)}, u32[]{:S(2)}, u32[]{:S(2)}) collective-permute-start(bf16[384,896]{1,0:T(8,128)(2,1)} %get-tuple-element.184), channel_id=1, source_target_pairs={{0,1},{1,0},{2,3},{3,2},{4,5},{5,4},{6,7},{7,6},{8,9},{9,8},{10,11... | collective-permute-start | bytes 2064392 | tf_op jit(solution)/shard_map/ppermute | solution.py:1103
  250.9 22.1 %collective-permute-start.21 = (bf16[96,3072]{1,0:T(8,128)(2,1)}, bf16[96,3072]{1,0:T(8,128)(2,1)}, u32[]{:S(2)}, u32[]{:S(2)}) collective-permute-start(bf16[96,3072]{1,0:T(8,128)(2,1)} %add_convert_fusion.4), channel_id=1, source_target_pairs={{0,8},{8,0},{16,24},{24,16},{1,9},{9,1},{17,25},{25,17},{2,10},{10... | collective-permute-start | bytes 1769480 | tf_op jit(solution)/shard_map/ppermute | solution.py:908
  253.9 20.6 %collective-permute-start.18 = (bf16[192,1536]{1,0:T(8,128)(2,1)}, bf16[192,1536]{1,0:T(8,128)(2,1)}, u32[]{:S(2)}, u32[]{:S(2)}) collective-permute-start(bf16[192,1536]{1,0:T(8,128)(2,1)} %add_convert_fusion.3), channel_id=1, source_target_pairs={{0,4},{4,0},{1,5},{5,1},{2,6},{6,2},{3,7},{7,3},{8,12},{12,8},{9,1... | collective-permute-start | bytes 1769480 | tf_op jit(solution)/shard_map/ppermute | solution.py:908
  267.0 8.8 %collective-permute-start.20 = (bf16[192,896]{1,0:T(8,128)(2,1)}, bf16[192,896]{1,0:T(8,128)(2,1)}, u32[]{:S(2)}, u32[]{:S(2)}) collective-permute-start(bf16[192,896]{1,0:T(8,128)(2,1)} %add_convert_fusion.6), channel_id=1, source_target_pairs={{0,4},{4,0},{1,5},{5,1},{2,6},{6,2},{3,7},{7,3},{8,12},{12,8},{9,1... | collective-permute-start | bytes 1032200 | tf_op jit(solution)/shard_map/ppermute | solution.py:908
  271.3 13.4 %collective-permute-start.24 = (bf16[384,768]{1,0:T(8,128)(2,1)}, bf16[384,768]{1,0:T(8,128)(2,1)S(1)}, u32[]{:S(2)}, u32[]{:S(2)}) collective-permute-start(bf16[384,768]{1,0:T(8,128)(2,1)} %get-tuple-element.192), channel_id=1, source_target_pairs={{0,1},{1,0},{2,3},{3,2},{4,5},{5,4},{6,7},{7,6},{8,9},{9,8},{10,11... | collective-permute-start | bytes 1769480 | tf_op jit(solution)/shard_map/ppermute | solution.py:1103
  274.5 12.1 %collective-permute-start.27 = (bf16[48,3072]{1,0:T(8,128)(2,1)S(1)}, bf16[48,3072]{1,0:T(8,128)(2,1)S(1)}, u32[]{:S(2)}, u32[]{:S(2)}) collective-permute-start(bf16[48,3072]{1,0:T(8,128)(2,1)S(1)} %add_convert_fusion.9), channel_id=1, source_target_pairs={{0,16},{8,24},{16,0},{24,8},{1,17},{9,25},{17,1},{25,9},{2,18},{10... | collective-permute-start | bytes 884744 | tf_op jit(solution)/shard_map/ppermute | solution.py:908
  278.6 15.1 %collective-permute-start.26 = (bf16[96,2432]{1,0:T(8,128)(2,1)S(1)}, bf16[96,2432]{1,0:T(8,128)(2,1)S(1)}, u32[]{:S(2)}, u32[]{:S(2)}) collective-permute-start(bf16[96,2432]{1,0:T(8,128)(2,1)S(1)} %fusion.2), channel_id=1, source_target_pairs={{0,8},{8,0},{16,24},{24,16},{1,9},{9,1},{17,25},{25,17},{2,10},{10... | collective-permute-start | bytes 1400840 | tf_op jit(solution)/shard_map/ppermute | solution.py:908
  279.0 9.1 %collective-permute-start.22 = (f32[128,768]{1,0:T(8,128)S(1)}, f32[128,768]{1,0:T(8,128)S(1)}, u32[]{:S(2)}, u32[]{:S(2)}) collective-permute-start(f32[128,768]{1,0:T(8,128)S(1)} %copy-done.33), channel_id=1, source_target_pairs={{0,2},{2,0},{1,3},{3,1},{4,6},{6,4},{5,7},{7,5},{8,10},{10,8},{9,1... | collective-permute-start | bytes 1179656 | tf_op jit(solution)/shard_map/ppermute | solution.py:885
  279.0 12.2 %collective-permute-start.23 = (f32[128,768]{1,0:T(8,128)}, f32[128,768]{1,0:T(8,128)S(1)}, u32[]{:S(2)}, u32[]{:S(2)}) collective-permute-start(f32[128,768]{1,0:T(8,128)} %get-tuple-element.200), channel_id=1, source_target_pairs={{0,2},{2,0},{1,3},{3,1},{4,6},{6,4},{5,7},{7,5},{8,10},{10,8},{9,1... | collective-permute-start | bytes 1179656 | tf_op jit(solution)/shard_map/ppermute | solution.py:885
  284.7 9.2 %collective-permute-start.25 = (bf16[192,768]{1,0:T(8,128)(2,1)S(1)}, bf16[192,768]{1,0:T(8,128)(2,1)S(1)}, u32[]{:S(2)}, u32[]{:S(2)}) collective-permute-start(bf16[192,768]{1,0:T(8,128)(2,1)S(1)} %add_convert_fusion.8), channel_id=1, source_target_pairs={{0,4},{4,0},{1,5},{5,1},{2,6},{6,2},{3,7},{7,3},{8,12},{12,8},{9,1... | collective-permute-start | bytes 884744 | tf_op jit(solution)/shard_map/ppermute | solution.py:908
  293.9 12.6 %collective-permute-start.29 = (bf16[48,2432]{1,0:T(8,128)(2,1)S(1)}, bf16[48,2432]{1,0:T(8,128)(2,1)S(1)}, u32[]{:S(2)}, u32[]{:S(2)}) collective-permute-start(bf16[48,2432]{1,0:T(8,128)(2,1)S(1)} %add_convert_fusion.11), channel_id=1, source_target_pairs={{0,16},{8,24},{16,0},{24,8},{1,17},{9,25},{17,1},{25,9},{2,18},{10... | collective-permute-start | bytes 700424 | tf_op jit(solution)/shard_map/ppermute | solution.py:908
  314.2 12.4 %collective-permute-start.30 = (bf16[48,768]{1,0:T(8,128)(2,1)S(1)}, bf16[48,768]{1,0:T(8,128)(2,1)S(1)}, u32[]{:S(2)}, u32[]{:S(2)}) collective-permute-start(bf16[48,768]{1,0:T(8,128)(2,1)S(1)} %add_convert_fusion.14), channel_id=1, source_target_pairs={{0,16},{8,24},{16,0},{24,8},{1,17},{9,25},{17,1},{25,9},{2,18},{10... | collective-permute-start | bytes 221192 | tf_op jit(solution)/shard_map/ppermute | solution.py:908
  327.7 13.1 %collective-permute-start.31 = (bf16[48,1664]{1,0:T(8,128)(2,1)S(1)}, bf16[48,1664]{1,0:T(8,128)(2,1)S(1)}, u32[]{:S(2)}, u32[]{:S(2)}) collective-permute-start(bf16[48,1664]{1,0:T(8,128)(2,1)S(1)} %pad_maximum_fusion.5), channel_id=1, source_target_pairs={{0,16},{8,24},{16,0},{24,8},{1,17},{9,25},{17,1},{25,9},{2,18},{10... | collective-permute-start | bytes 479240 | tf_op jit(solution)/shard_map/ppermute | solution.py:908
  340.8 21.1 %collective-permute-start.32 = (bf16[96,1664]{1,0:T(8,128)(2,1)S(1)}, bf16[96,1664]{1,0:T(8,128)(2,1)S(1)}, u32[]{:S(2)}, u32[]{:S(2)}) collective-permute-start(bf16[96,1664]{1,0:T(8,128)(2,1)S(1)} %pad_maximum_fusion.4), channel_id=1, source_target_pairs={{0,8},{8,0},{16,24},{24,16},{1,9},{9,1},{17,25},{25,17},{2,10},{10... | collective-permute-start | bytes 958472 | tf_op jit(solution)/shard_map/ppermute | solution.py:908
  362.0 16.9 %collective-permute-start.33 = (bf16[192,1664]{1,0:T(8,128)(2,1)S(1)}, bf16[192,1664]{1,0:T(8,128)(2,1)S(1)}, u32[]{:S(2)}, u32[]{:S(2)}) collective-permute-start(bf16[192,1664]{1,0:T(8,128)(2,1)S(1)} %pad_maximum_fusion.1), channel_id=1, source_target_pairs={{0,4},{4,0},{1,5},{5,1},{2,6},{6,2},{3,7},{7,3},{8,12},{12,8},{9,1... | collective-permute-start | bytes 1916936 | tf_op jit(solution)/shard_map/ppermute | solution.py:908
  (42 other events, 302.0 us)
Sparse Core Ops, SparseCore 0:
  10.9 64.5 all-gather.5
  158.8 52.7 all-gather.7
  213.9 36.6 reduce-scatter.1
  307.5 86.0 all-gather.9

commit v2 on v1

--- a/solution.py
+++ b/solution.py
@@ -1147,16 +1147,16 @@
     first_got = swap_bit(first_sent, *z_near)
     second_keep, second_sent = parted(after(second, first_sent), *y_steps[0])
     second_got = swap_bit(second_sent, *y_steps[0])
-    fourth_keep, fourth_sent = parted(after(fourth, second_sent), *y_steps[0])
-    fourth_got = swap_bit(fourth_sent, *y_steps[0])
     enc_keep, enc_send, *third = call(
-        functools.partial(encoder_grads_kernel, n_fsdp), (at,), (after(dkv_cross, fourth_sent), e_chip, w_cross),
+        functools.partial(encoder_grads_kernel, n_fsdp), (at,), (after(dkv_cross, second_sent), e_chip, w_cross),
         [half_rows, half_rows, *given(2 * HALF)],
         [((ROWS, 2 * HALF), BF16), wide, ((width, 2 * HALF), BF16)], 8 * ROWS * width * HALF,
     )
     third_sent = third[-1]
     third = over_fsdp(third)
-    first_keep, first_sent = parted(first_keep + [after(first_got, third_sent)], *z_far)
+    fourth_keep, fourth_sent = parted(after(fourth, third_sent), *y_steps[0])
+    fourth_got = swap_bit(fourth_sent, *y_steps[0])
+    first_keep, first_sent = parted(first_keep + [after(first_got, fourth_sent)], *z_far)
     first_got = swap_bit(first_sent, *z_far)
 
     second_got, fourth_got = after((second_got, fourth_got), first_sent)

time: 415 us -> 409 us (0.986)
  waiting for transfers between devices: 190 us -> 177 us
  starting transfers between devices: 23.4 us -> 30.7 us
    ppermute x14, starting transfers between devices: 6.35 us -> 13.6 us  [swap_bit(): lax.ppermute(value, axis, [(i, i ^ 1 << bit) for i in range(lax.axis_size...]
    ppermute x3, waiting for transfers between devices: 16.3 us -> 9.32 us  [over_fsdp(): return [parts[0], lax.ppermute(parts[1], 'fsdp', [(0, 1), (1, 0)])]]
    ppermute x14, waiting for transfers between devices: 109 us -> 105 us  [swap_bit(): lax.ppermute(value, axis, [(i, i ^ 1 << bit) for i in range(lax.axis_size...]
    unnamed x79 -> x81, local copies, waits for them, and re-layouts: 9.59 us -> 9.63 us
where the time goes in v2:
time: 409 us; the launch traced here: 403 us
  waiting for transfers between devices  177 us (43%)
  Pallas kernels  136 us (33%)
  starting transfers between devices  30.7 us (8%)
  other arithmetic  26.8 us (7%)
  local copies, waits for them, and re-layouts  15.4 us (4%)
  between operations  14.8 us (4%)
    pallas_call x14, Pallas kernels, call(): pl.pallas_call(kernel, out_shape=[jax.ShapeDtypeStruct(s, d) for s, d in...  129 us
    ppermute x14, waiting for transfers between devices, swap_bit(): lax.ppermute(value, axis, [(i, i ^ 1 << bit) for i in range(lax.axis_size...  105 us
    ppermute x6, waiting for transfers between devices, gather_fsdp(): return [own, lax.ppermute(own, 'fsdp', [(0, 1), (1, 0)])]  40.1 us
    ppermute x14, starting transfers between devices, swap_bit(): lax.ppermute(value, axis, [(i, i ^ 1 << bit) for i in range(lax.axis_size...  13.6 us
    convert_element_type x9, other arithmetic, parted(): return (half(side), total(half(1 - side)).astype(BF16))  11.7 us
    unnamed x81, local copies, waits for them, and re-layouts  9.63 us
    ppermute x3, waiting for transfers between devices, over_fsdp(): return [parts[0], lax.ppermute(parts[1], 'fsdp', [(0, 1), (1, 0)])]  9.32 us
    ppermute x6, starting transfers between devices, gather_fsdp(): return [own, lax.ppermute(own, 'fsdp', [(0, 1), (1, 0)])]  9.3 us
  transfers between devices with their start and end apart: 39, of which 24 were waited for; matrix products, arithmetic and copies ran while one was open for 8% of the time, Pallas kernels for 24%

profile of v2, /device:TPU:0, one launch (start us, length us, event | category | flops | bytes accessed | tf_op | source)
XLA Modules:
  0.0 403.3 jit_solution(17645770566174002569)
XLA Ops:
  9.2 5.3 %shard_map.362 = (bf16[384,768]{1,0:T(8,128)(2,1)}, bf16[384,1152]{1,0:T(8,128)(2,1)}, bf16[384,1536]{1,0:T(8,128)(2,1)}, bf16[768,768]{1,0:T(8,128)(2,1)}) custom-call(s32[1]{0:T(128)} %bitcast.1.core_ref, f32[384,768]{1,0:T(8,128)} %refs_0_.3, f32[384,768]{1,0:T(8,128)} %refs_1_.3, f32[384,768]{1,0:T(8,128)} %refs_2_.3, f32[384,768]{1,0:T(8,128)} %refs_3_.1, ...), custom_call_target="tpu_custom_call" | custom-call | tf_op jit(solution)/shard_map/pallas_call | solution.py:867
  14.4 2.9 collective-permute-start.6
  22.4 15.7 %collective-permute-done.6.refs_5_ = bf16[384,1152]{1,0:T(8,128)(2,1)S(1)} collective-permute-done((bf16[384,1152]{1,0:T(8,128)(2,1)}, bf16[384,1152]{1,0:T(8,128)(2,1)S(1)}, u32[]{:S(2)}, u32[]{:S(2)}) %collective-permute-start.6) | collective-permute-done | bytes 884768 | tf_op jit(solution)/shard_map/ppermute | solution.py:892
  41.0 9.8 %collective-permute-done = bf16[1,1344]{1,0:T(2,128)(2,1)S(1)} collective-permute-done((bf16[1,1344]{1,0:T(2,128)(2,1)S(1)}, bf16[1,1344]{1,0:T(2,128)(2,1)S(1)}, u32[]{:S(2)}, u32[]{:S(2)}) %collective-permute-start) | collective-permute-done | bytes 2720 | tf_op jit(solution)/shard_map/ppermute | solution.py:892
  58.3 3.8 shard_map.359.tiles
  62.8 7.1 %collective-permute-done.1.refs_1_ = bf16[384,1152]{1,0:T(8,128)(2,1)} collective-permute-done((bf16[384,1152]{1,0:T(8,128)(2,1)}, bf16[384,1152]{1,0:T(8,128)(2,1)}, u32[]{:S(2)}, u32[]{:S(2)}) %collective-permute-start.1) | collective-permute-done | bytes 884768 | tf_op jit(solution)/shard_map/ppermute | solution.py:892
  69.9 5.6 %all-gather.6.cloned.1.call-done.xe_ref = bf16[2048,1536]{1,0:T(8,128)(2,1)} async-done(((bf16[128,1536]{1,0:T(8,128)(2,1)}), bf16[2048,1536]{1,0:T(8,128)(2,1)}) %all-gather.6.cloned.1.call-update) | async-done | bytes 6291472 | tf_op jit(solution)/shard_map/all_gather | solution.py:900
  75.5 14.3 %shard_map.361 = (bf16[9,2048,128]{2,1,0:T(8,128)(2,1)}, bf16[768,1152]{1,0:T(8,128)(2,1)}, f32[256,384]{1,0:T(8,128)}, bf16[256,384]{1,0:T(8,128)(2,1)}, f32[256,128]{1,0:T(8,128)}) custom-call(s32[4]{0:T(128)} %pad_add_fusion.at_ref, s32[1,6]{1,0:T(1,128)} %len_ref.9, bf16[2048,1536]{1,0:T(8,128)(2,1)} %all-gather.6.cloned.1.call-done.xe_ref, ...), custom_call_target="tpu_custom_call" | custom-call | flops 1 | bytes 1 | tf_op jit(solution)/shard_map/pallas_call | solution.py:847
  92.1 19.1 %shard_map.363 = (f32[256,768]{1,0:T(8,128)}, bf16[256,768]{1,0:T(8,128)(2,1)}, bf16[256,384]{1,0:T(8,128)(2,1)}, bf16[6,2048,128]{2,1,0:T(8,128)(2,1)}, f32[256...) custom-call(s32[4]{0:T(128)} %pad_add_fusion.at_ref, ...), custom_call_target="tpu_custom_call" | custom-call | flops 1 | bytes 1 | tf_op jit(solution)/shard_map/pallas_call | solution.py:847
  112.1 7.5 %collective-permute-done.10.refs_3_ = bf16[768,768]{1,0:T(8,128)(2,1)} collective-permute-done((bf16[768,768]{1,0:T(8,128)(2,1)S(1)}, bf16[768,768]{1,0:T(8,128)(2,1)}, u32[]{:S(2)}, u32[]{:S(2)}) %collective-permute-start.10) | collective-permute-done | bytes 1179680 | tf_op jit(solution)/shard_map/ppermute | solution.py:892
  120.3 8.7 %shard_map.364 = (f32[256,768]{1,0:T(8,128)}, bf16[256,768]{1,0:T(8,128)(2,1)}, bf16[256,1536]{1,0:T(8,128)(2,1)}, bf16[256,1536]{1,0:T(8,128)(2,1)}, bf16[256,7...) custom-call(s32[4]{0:T(128)} %pad_add_fusion.at_ref, ...), custom_call_target="tpu_custom_call" | custom-call | flops 1 | bytes 1 | tf_op jit(solution)/shard_map/pallas_call | solution.py:847
  132.4 18.8 %shard_map.365 = (f32[256,768]{1,0:T(8,128)}, bf16[256,768]{1,0:T(8,128)(2,1)}, f32[1,768]{1,0:T(1,128)}, bf16[256,384]{1,0:T(8,128)(2,1)}, bf16[1024,768]{1,0:T...) custom-call(s32[4]{0:T(128)} %pad_add_fusion.at_ref, s32[1,6]{1,0:T(1,128)} %len_ref.9, s32[1,6]{1,0:T(1,128)} %enc_ref.3, ...), custom_call_target="tpu_custom_call" | custom-call | flops 1 | bytes 1 | tf_op jit(solution)/shard_map/pallas_call | solution.py:847
  154.5 4.2 %shard_map.366 = (f32[256,768]{1,0:T(8,128)}, bf16[256,768]{1,0:T(8,128)(2,1)}, f32[1,768]{1,0:T(1,128)}, bf16[256,384]{1,0:T(8,128)(2,1)}, bf16[144,768]{1,0:T(8,128)(2,1)}) custom-call(s32[4]{0:T(128)} %pad_add_fusion.at_ref, f32[256,768]{1,0:T(8,128)} %get-tuple-element.148.e_ref, f32[256,768]{1,0:T(8,128)} %copy-done.11, ...), custom_call_target="tpu_custom_call" | custom-call | flops 1 | bytes 1 | tf_op jit(solution)/shard_map/pallas_call | solution.py:847
  158.9 5.7 %shard_map.367 = (bf16[384,3072]{1,0:T(8,128)(2,1)}, bf16[384,3072]{1,0:T(8,128)(2,1)}) custom-call(s32[4]{0:T(128)} %pad_add_fusion.at_ref, bf16[256,1536]{1,0:T(8,128)(2,1)} %get-tuple-element.154.hid_ref, bf16[256,768]{1,0:T(8,128)(2,1)} %get-tuple-element.142.cot_ref, bf16[256,768]{1,0:T(8,128)(2,1)} %get-tuple-element.155.in_ref, ...), custom_call_target="tpu_custom_call" | custom-call | flops 1 | bytes 1 | tf_op jit(solution)/shard_map/pallas_call | solution.py:847
  168.4 9.4 %shard_map.368 = (bf16[256,384]{1,0:T(8,128)(2,1)}, f32[8,512]{1,0:T(8,128)}) custom-call(s32[4]{0:T(128)} %pad_add_fusion.at_ref, s32[1,6]{1,0:T(1,128)} %len_ref.9, bf16[2,3,6,256,256]{4,3,2,1,0:T(8,128)(2,1)} %shard_map.359.tiles, bf16[9,2048,128]{2,1,0:T(8,128)(2,1)} %get-tuple-element.139.qkv_ref, bf16[256,384]{1,0:T(8,128)(2,1)} %get-tuple-element.167.go_ref, ...), custom_call_target="tpu_custom_call" | custom-call | flops 1 | bytes 1 | tf_op jit(solution)/shard_map/pallas_call | solution.py:847
  177.9 4.4 %shard_map.369 = (bf16[384,1536]{1,0:T(8,128)(2,1)}, bf16[384,1536]{1,0:T(8,128)(2,1)}) custom-call(s32[4]{0:T(128)} %pad_add_fusion.at_ref, bf16[256,384]{1,0:T(8,128)(2,1)} %get-tuple-element.131.low_ref.low2_ref, bf16[256,384]{1,0:T(8,128)(2,1)} %copy-done.12, bf16[256,768]{1,0:T(8,128)(2,1)} %get-tuple-element.162.b2_ref, ...), custom_call_target="tpu_custom_call" | custom-call | flops 1 | bytes 1 | tf_op jit(solution)/shard_map/pallas_call | solution.py:847
  182.2 24.9 %collective-permute-done.15 = bf16[1024,768]{1,0:T(8,128)(2,1)S(1)} collective-permute-done((bf16[1024,768]{1,0:T(8,128)(2,1)S(1)}, bf16[1024,768]{1,0:T(8,128)(2,1)S(1)}, u32[]{:S(2)}, u32[]{:S(2)}) %collective-permute-start.15) | collective-permute-done | bytes 1572896 | tf_op jit(solution)/shard_map/ppermute | solution.py:908
  208.4 3.1 add_convert_fusion
  211.6 6.6 %collective-permute-done.14 = bf16[384,3072]{1,0:T(8,128)(2,1)} collective-permute-done((bf16[384,3072]{1,0:T(8,128)(2,1)}, bf16[384,3072]{1,0:T(8,128)(2,1)}, u32[]{:S(2)}, u32[]{:S(2)}) %collective-permute-start.14) | collective-permute-done | bytes 2359328 | tf_op jit(solution)/shard_map/ppermute | solution.py:1087
  227.3 20.7 %shard_map.370 = (f32[128,768]{1,0:T(8,128)}, f32[128,768]{1,0:T(8,128)}, bf16[384,896]{1,0:T(8,128)(2,1)}, bf16[384,896]{1,0:T(8,128)(2,1)}) custom-call(s32[4]{0:T(128)} %pad_add_fusion.at_ref, s32[1,6]{1,0:T(1,128)} %len_ref.9, bf16[2,3,6,256,256]{4,3,2,1,0:T(8,128)(2,1)} %shard_map.359.tiles, bf16[9,2048,128]{2,1,0:T(8,128)(2,1)} %get-tuple-element.139.qkv_ref, ...), custom_call_target="tpu_custom_call" | custom-call | flops 1 | bytes 1 | tf_op jit(solution)/shard_map/pallas_call | solution.py:847
  255.0 3.7 shard_map.371
  258.7 6.4 %collective-permute-done.19 = bf16[384,896]{1,0:T(8,128)(2,1)} collective-permute-done((bf16[384,896]{1,0:T(8,128)(2,1)}, bf16[384,896]{1,0:T(8,128)(2,1)}, u32[]{:S(2)}, u32[]{:S(2)}) %collective-permute-start.19) | collective-permute-done | bytes 688160 | tf_op jit(solution)/shard_map/ppermute | solution.py:1103
  270.8 4.9 %collective-permute-done.20 = bf16[192,896]{1,0:T(8,128)(2,1)} collective-permute-done((bf16[192,896]{1,0:T(8,128)(2,1)}, bf16[192,896]{1,0:T(8,128)(2,1)}, u32[]{:S(2)}, u32[]{:S(2)}) %collective-permute-start.20) | collective-permute-done | bytes 344096 | tf_op jit(solution)/shard_map/ppermute | solution.py:908
  290.4 10.3 %collective-permute-done.29 = bf16[48,2432]{1,0:T(8,128)(2,1)S(1)} collective-permute-done((bf16[48,2432]{1,0:T(8,128)(2,1)S(1)}, bf16[48,2432]{1,0:T(8,128)(2,1)S(1)}, u32[]{:S(2)}, u32[]{:S(2)}) %collective-permute-start.29) | collective-permute-done | bytes 233504 | tf_op jit(solution)/shard_map/ppermute | solution.py:908
  301.7 5.2 %collective-permute-done.28 = bf16[96,768]{1,0:T(8,128)(2,1)S(1)} collective-permute-done((bf16[96,768]{1,0:T(8,128)(2,1)S(1)}, bf16[96,768]{1,0:T(8,128)(2,1)S(1)}, u32[]{:S(2)}, u32[]{:S(2)}) %collective-permute-start.28) | collective-permute-done | bytes 147488 | tf_op jit(solution)/shard_map/ppermute | solution.py:908
  307.9 11.3 %collective-permute-done.30 = bf16[48,768]{1,0:T(8,128)(2,1)S(1)} collective-permute-done((bf16[48,768]{1,0:T(8,128)(2,1)S(1)}, bf16[48,768]{1,0:T(8,128)(2,1)S(1)}, u32[]{:S(2)}, u32[]{:S(2)}) %collective-permute-start.30) | collective-permute-done | bytes 73760 | tf_op jit(solution)/shard_map/ppermute | solution.py:908
  320.3 13.4 %collective-permute-done.31 = bf16[48,1664]{1,0:T(8,128)(2,1)S(1)} collective-permute-done((bf16[48,1664]{1,0:T(8,128)(2,1)S(1)}, bf16[48,1664]{1,0:T(8,128)(2,1)S(1)}, u32[]{:S(2)}, u32[]{:S(2)}) %collective-permute-start.31) | collective-permute-done | bytes 159776 | tf_op jit(solution)/shard_map/ppermute | solution.py:908
  333.8 7.3 %collective-permute-done.32 = bf16[96,1664]{1,0:T(8,128)(2,1)S(1)} collective-permute-done((bf16[96,1664]{1,0:T(8,128)(2,1)S(1)}, bf16[96,1664]{1,0:T(8,128)(2,1)S(1)}, u32[]{:S(2)}, u32[]{:S(2)}) %collective-permute-start.32) | collective-permute-done | bytes 319520 | tf_op jit(solution)/shard_map/ppermute | solution.py:908
  341.2 7.6 %collective-permute-start.33 = (bf16[192,1664]{1,0:T(8,128)(2,1)S(1)}, bf16[192,1664]{1,0:T(8,128)(2,1)S(1)}, u32[]{:S(2)}, u32[]{:S(2)}) collective-permute-start(bf16[192,1664]{1,0:T(8,128)(2,1)S(1)} %pad_maximum_fusion.1), channel_id=1, source_target_pairs={{0,4},{4,0},{1,5},{5,1},{2,6},{6,2},{3,7},{7,3},{8,12},{12,8},{9,1... | collective-permute-start | bytes 1916936 | tf_op jit(solution)/shard_map/ppermute | solution.py:908
  348.8 26.0 %collective-permute-done.33 = bf16[192,1664]{1,0:T(8,128)(2,1)S(1)} collective-permute-done((bf16[192,1664]{1,0:T(8,128)(2,1)S(1)}, bf16[192,1664]{1,0:T(8,128)(2,1)S(1)}, u32[]{:S(2)}, u32[]{:S(2)}) %collective-permute-start.33) | collective-permute-done | bytes 639008 | tf_op jit(solution)/shard_map/ppermute | solution.py:908
  380.7 5.0 %shard_map.373 = (f32[384,768]{1,0:T(8,128)}, f32[384,768]{1,0:T(8,128)}, f32[384,768]{1,0:T(8,128)}, f32[384,768]{1,0:T(8,128)}, f32[384]{0:T(512)}, /*index=5*/f32[384]{0:T(512)}, f32[384]{0:T(512)}, f32[16,12]{1,0:T(8,128)}) custom-call(s32[4]{0:T(128)} %pad_add_fusion.at_ref, s32[1]{0:T(128)} %dynamic_slice.198.place_ref, bf16[384,1664]{1,0:T(8,128)(2,1)} %copy-done, ...), custom_call_target="tpu_custom_call" | custom-call | flops 1 | bytes 1 | tf_op jit(solution)/shard_map/pallas_call | solution.py:847
  388.0 8.4 %shard_map.374 = (f32[1536,768]{1,0:T(8,128)}, f32[384,3072]{1,0:T(8,128)}, f32[384,768]{1,0:T(8,128)}, f32[384,768]{1,0:T(8,128)}, f32[384,768]{1,0:T(8,128)}, /*index=5*/f32[384,768]{1,0:T(8,128)}) custom-call(bf16[16,48,4608]{2,1,0:T(8,128)(2,1)} %bitcast.45), custom_call_target="tpu_custom_call" | custom-call | flops 1 | bytes 1 | tf_op jit(solution)/shard_map/pallas_call | solution.py:847
  (198 shorter events, 81.5 us)
Async XLA Ops:
  7.2 68.3 %all-gather.6.cloned.1.call-start = ((), (), s32[]{:S(2)}) async-start(), calls=%async_computation.1 | async-start | bytes 6684672 | tf_op jit(solution)/shard_map/all_gather | solution.py:900
  9.1 218.2 %all-gather.8.cloned.1.call-start = ((), (), s32[]{:S(2)}) async-start(), calls=%async_computation.3 | async-start | bytes 3760128 | tf_op jit(solution)/shard_map/all_gather | solution.py:1089
  14.4 23.6 %collective-permute-start.6 = (bf16[384,1152]{1,0:T(8,128)(2,1)}, bf16[384,1152]{1,0:T(8,128)(2,1)S(1)}, u32[]{:S(2)}, u32[]{:S(2)}) collective-permute-start(bf16[384,1152]{1,0:T(8,128)(2,1)} %get-tuple-element.129.refs_4_), channel_id=1, source_target_pairs={{0,1},{1,0},{2,3},{3,2},{4,5},{5,4},{6,7},{7,6},{8,9},{9,8},{10,11... | collective-permute-start | bytes 2654216 | tf_op jit(solution)/shard_map/ppermute | solution.py:892
  17.4 39.7 %collective-permute-start.3 = (bf16[384,768]{1,0:T(8,128)(2,1)}, bf16[384,768]{1,0:T(8,128)(2,1)}, u32[]{:S(2)}, u32[]{:S(2)}) collective-permute-start(bf16[384,768]{1,0:T(8,128)(2,1)} %get-tuple-element.128.refs_0_), channel_id=1, source_target_pairs={{0,1},{1,0},{2,3},{3,2},{4,5},{5,4},{6,7},{7,6},{8,9},{9,8},{10,11... | collective-permute-start | bytes 1769480 | tf_op jit(solution)/shard_map/ppermute | solution.py:892
  17.7 33.2 %collective-permute-start = (bf16[1,1344]{1,0:T(2,128)(2,1)S(1)}, bf16[1,1344]{1,0:T(2,128)(2,1)S(1)}, u32[]{:S(2)}, u32[]{:S(2)}) collective-permute-start(bf16[1,1344]{1,0:T(2,128)(2,1)S(1)} %constant_dynamic-update-slice_fusion), channel_id=1, source_target_pairs={{0,1},{1,0},{2,3},{3,2},{4,5},{5,4},{6,7},{7,6},{8,9},{9,8},{10,11... | collective-permute-start | bytes 8072 | tf_op jit(solution)/shard_map/ppermute | solution.py:892
  19.7 70.9 %collective-permute-start.4 = (bf16[384,768]{1,0:T(8,128)(2,1)}, bf16[384,768]{1,0:T(8,128)(2,1)}, u32[]{:S(2)}, u32[]{:S(2)}) collective-permute-start(bf16[384,768]{1,0:T(8,128)(2,1)} %get-tuple-element.128.refs_0_), channel_id=1, source_target_pairs={{0,2},{2,0},{1,3},{3,1},{4,6},{6,4},{5,7},{7,5},{8,10},{10,8},{9,1... | collective-permute-start | bytes 1769480 | tf_op jit(solution)/shard_map/ppermute | solution.py:885
  22.2 47.7 %collective-permute-start.1 = (bf16[384,1152]{1,0:T(8,128)(2,1)}, bf16[384,1152]{1,0:T(8,128)(2,1)}, u32[]{:S(2)}, u32[]{:S(2)}) collective-permute-start(bf16[384,1152]{1,0:T(8,128)(2,1)} %shard_map.360.refs_0_), channel_id=1, source_target_pairs={{0,1},{1,0},{2,3},{3,2},{4,5},{5,4},{6,7},{7,6},{8,9},{9,8},{10,11... | collective-permute-start | bytes 2654216 | tf_op jit(solution)/shard_map/ppermute | solution.py:892
  39.0 73.1 %collective-permute-start.9 = (bf16[384,1536]{1,0:T(8,128)(2,1)S(1)}, bf16[384,1536]{1,0:T(8,128)(2,1)S(1)}, u32[]{:S(2)}, u32[]{:S(2)}) collective-permute-start(bf16[384,1536]{1,0:T(8,128)(2,1)S(1)} %copy-done.6), channel_id=1, source_target_pairs={{0,1},{1,0},{2,3},{3,2},{4,5},{5,4},{6,7},{7,6},{8,9},{9,8},{10,11... | collective-permute-start | bytes 3538952 | tf_op jit(solution)/shard_map/ppermute | solution.py:892
  51.4 68.2 %collective-permute-start.10 = (bf16[768,768]{1,0:T(8,128)(2,1)S(1)}, bf16[768,768]{1,0:T(8,128)(2,1)}, u32[]{:S(2)}, u32[]{:S(2)}) collective-permute-start(bf16[768,768]{1,0:T(8,128)(2,1)S(1)} %copy-done.7), channel_id=1, source_target_pairs={{0,1},{1,0},{2,3},{3,2},{4,5},{5,4},{6,7},{7,6},{8,9},{9,8},{10,11... | collective-permute-start | bytes 3538952 | tf_op jit(solution)/shard_map/ppermute | solution.py:892
  57.1 33.8 %collective-permute-start.5 = (bf16[384,768]{1,0:T(8,128)(2,1)}, bf16[384,768]{1,0:T(8,128)(2,1)}, u32[]{:S(2)}, u32[]{:S(2)}) collective-permute-start(bf16[384,768]{1,0:T(8,128)(2,1)} %collective-permute-done.3.refs_1_), channel_id=1, source_target_pairs={{0,2},{2,0},{1,3},{3,1},{4,6},{6,4},{5,7},{7,5},{8,10},{10,8},{9,1... | collective-permute-start | bytes 1769480 | tf_op jit(solution)/shard_map/ppermute | solution.py:885
  90.6 21.5 %collective-permute-start.8 = (bf16[128,768]{1,0:T(8,128)(2,1)S(1)}, bf16[128,768]{1,0:T(8,128)(2,1)S(1)}, u32[]{:S(2)}, u32[]{:S(2)}) collective-permute-start(bf16[128,768]{1,0:T(8,128)(2,1)S(1)} %copy-done.22), channel_id=1, source_target_pairs={{0,2},{2,0},{1,3},{3,1},{4,6},{6,4},{5,7},{7,5},{8,10},{10,8},{9,1... | collective-permute-start | bytes 589832 | tf_op jit(solution)/shard_map/ppermute | solution.py:885
  111.2 8.4 %collective-permute-start.7 = (bf16[256,384]{1,0:T(8,128)(2,1)}, bf16[256,384]{1,0:T(8,128)(2,1)S(1)}, u32[]{:S(2)}, u32[]{:S(2)}) collective-permute-start(bf16[256,384]{1,0:T(8,128)(2,1)} %get-tuple-element.131.low_ref.low2_ref), channel_id=1, source_target_pairs={{0,2},{2,0},{1,3},{3,1},{4,6},{6,4},{5,7},{7,5},{8,10},{10,8},{9,1... | collective-permute-start | bytes 589832 | tf_op jit(solution)/shard_map/ppermute | solution.py:885
  158.7 96.2 %reduce-scatter.2.cloned.1.call-start = ((), (), s32[]{:S(2)}) async-start(), calls=%async_computation.2 | async-start | bytes 1966080 | tf_op jit(solution)/shard_map/reduce_scatter | solution.py:1131
  158.8 48.4 %collective-permute-start.15 = (bf16[1024,768]{1,0:T(8,128)(2,1)S(1)}, bf16[1024,768]{1,0:T(8,128)(2,1)S(1)}, u32[]{:S(2)}, u32[]{:S(2)}) collective-permute-start(bf16[1024,768]{1,0:T(8,128)(2,1)S(1)} %copy-done.33), channel_id=1, source_target_pairs={{0,4},{4,0},{1,5},{5,1},{2,6},{6,2},{3,7},{7,3},{8,12},{12,8},{9,1... | collective-permute-start | bytes 4718600 | tf_op jit(solution)/shard_map/ppermute | solution.py:908
  164.6 53.6 %collective-permute-start.14 = (bf16[384,3072]{1,0:T(8,128)(2,1)}, bf16[384,3072]{1,0:T(8,128)(2,1)}, u32[]{:S(2)}, u32[]{:S(2)}) collective-permute-start(bf16[384,3072]{1,0:T(8,128)(2,1)} %get-tuple-element.159), channel_id=1, source_target_pairs={{0,1},{1,0},{2,3},{3,2},{4,5},{5,4},{6,7},{7,6},{8,9},{9,8},{10,11... | collective-permute-start | bytes 7077896 | tf_op jit(solution)/shard_map/ppermute | solution.py:1087
  211.6 176.4 %all-gather.10.cloned.1.call-start = ((), (), s32[]{:S(2)}) async-start(), calls=%async_computation.4 | async-start | bytes 7520256 | tf_op jit(solution)/shard_map/all_gather | solution.py:1183
  221.0 27.5 %collective-permute-start.17 = (bf16[192,3072]{1,0:T(8,128)(2,1)}, bf16[192,3072]{1,0:T(8,128)(2,1)}, u32[]{:S(2)}, u32[]{:S(2)}) collective-permute-start(bf16[192,3072]{1,0:T(8,128)(2,1)} %add_convert_fusion.1), channel_id=1, source_target_pairs={{0,4},{4,0},{1,5},{5,1},{2,6},{6,2},{3,7},{7,3},{8,12},{12,8},{9,1... | collective-permute-start | bytes 3538952 | tf_op jit(solution)/shard_map/ppermute | solution.py:908
  223.4 28.5 %collective-permute-start.16 = (bf16[384,1536]{1,0:T(8,128)(2,1)}, bf16[384,1536]{1,0:T(8,128)(2,1)}, u32[]{:S(2)}, u32[]{:S(2)}) collective-permute-start(bf16[384,1536]{1,0:T(8,128)(2,1)} %get-tuple-element.183), channel_id=1, source_target_pairs={{0,1},{1,0},{2,3},{3,2},{4,5},{5,4},{6,7},{7,6},{8,9},{9,8},{10,11... | collective-permute-start | bytes 3538952 | tf_op jit(solution)/shard_map/ppermute | solution.py:1103
  248.0 17.1 %collective-permute-start.19 = (bf16[384,896]{1,0:T(8,128)(2,1)}, bf16[384,896]{1,0:T(8,128)(2,1)}, u32[]{:S(2)}, u32[]{:S(2)}) collective-permute-start(bf16[384,896]{1,0:T(8,128)(2,1)} %get-tuple-element.184), channel_id=1, source_target_pairs={{0,1},{1,0},{2,3},{3,2},{4,5},{5,4},{6,7},{7,6},{8,9},{9,8},{10,11... | collective-permute-start | bytes 2064392 | tf_op jit(solution)/shard_map/ppermute | solution.py:1103
  250.9 18.3 %collective-permute-start.21 = (bf16[96,3072]{1,0:T(8,128)(2,1)}, bf16[96,3072]{1,0:T(8,128)(2,1)}, u32[]{:S(2)}, u32[]{:S(2)}) collective-permute-start(bf16[96,3072]{1,0:T(8,128)(2,1)} %add_convert_fusion.4), channel_id=1, source_target_pairs={{0,8},{8,0},{16,24},{24,16},{1,9},{9,1},{17,25},{25,17},{2,10},{10... | collective-permute-start | bytes 1769480 | tf_op jit(solution)/shard_map/ppermute | solution.py:908
  253.9 16.8 %collective-permute-start.18 = (bf16[192,1536]{1,0:T(8,128)(2,1)}, bf16[192,1536]{1,0:T(8,128)(2,1)}, u32[]{:S(2)}, u32[]{:S(2)}) collective-permute-start(bf16[192,1536]{1,0:T(8,128)(2,1)} %add_convert_fusion.3), channel_id=1, source_target_pairs={{0,4},{4,0},{1,5},{5,1},{2,6},{6,2},{3,7},{7,3},{8,12},{12,8},{9,1... | collective-permute-start | bytes 1769480 | tf_op jit(solution)/shard_map/ppermute | solution.py:908
  266.9 8.8 %collective-permute-start.20 = (bf16[192,896]{1,0:T(8,128)(2,1)}, bf16[192,896]{1,0:T(8,128)(2,1)}, u32[]{:S(2)}, u32[]{:S(2)}) collective-permute-start(bf16[192,896]{1,0:T(8,128)(2,1)} %add_convert_fusion.6), channel_id=1, source_target_pairs={{0,4},{4,0},{1,5},{5,1},{2,6},{6,2},{3,7},{7,3},{8,12},{12,8},{9,1... | collective-permute-start | bytes 1032200 | tf_op jit(solution)/shard_map/ppermute | solution.py:908
  267.5 13.4 %collective-permute-start.24 = (bf16[384,768]{1,0:T(8,128)(2,1)}, bf16[384,768]{1,0:T(8,128)(2,1)S(1)}, u32[]{:S(2)}, u32[]{:S(2)}) collective-permute-start(bf16[384,768]{1,0:T(8,128)(2,1)} %get-tuple-element.190), channel_id=1, source_target_pairs={{0,1},{1,0},{2,3},{3,2},{4,5},{5,4},{6,7},{7,6},{8,9},{9,8},{10,11... | collective-permute-start | bytes 1769480 | tf_op jit(solution)/shard_map/ppermute | solution.py:1103
  270.7 12.1 %collective-permute-start.27 = (bf16[48,3072]{1,0:T(8,128)(2,1)S(1)}, bf16[48,3072]{1,0:T(8,128)(2,1)S(1)}, u32[]{:S(2)}, u32[]{:S(2)}) collective-permute-start(bf16[48,3072]{1,0:T(8,128)(2,1)S(1)} %add_convert_fusion.9), channel_id=1, source_target_pairs={{0,16},{8,24},{16,0},{24,8},{1,17},{9,25},{17,1},{25,9},{2,18},{10... | collective-permute-start | bytes 884744 | tf_op jit(solution)/shard_map/ppermute | solution.py:908
  278.5 11.5 %collective-permute-start.26 = (bf16[96,2432]{1,0:T(8,128)(2,1)S(1)}, bf16[96,2432]{1,0:T(8,128)(2,1)S(1)}, u32[]{:S(2)}, u32[]{:S(2)}) collective-permute-start(bf16[96,2432]{1,0:T(8,128)(2,1)S(1)} %fusion.2), channel_id=1, source_target_pairs={{0,8},{8,0},{16,24},{24,16},{1,9},{9,1},{17,25},{25,17},{2,10},{10... | collective-permute-start | bytes 1400840 | tf_op jit(solution)/shard_map/ppermute | solution.py:908
  280.9 9.3 %collective-permute-start.25 = (bf16[192,768]{1,0:T(8,128)(2,1)S(1)}, bf16[192,768]{1,0:T(8,128)(2,1)S(1)}, u32[]{:S(2)}, u32[]{:S(2)}) collective-permute-start(bf16[192,768]{1,0:T(8,128)(2,1)S(1)} %add_convert_fusion.8), channel_id=1, source_target_pairs={{0,4},{4,0},{1,5},{5,1},{2,6},{6,2},{3,7},{7,3},{8,12},{12,8},{9,1... | collective-permute-start | bytes 884744 | tf_op jit(solution)/shard_map/ppermute | solution.py:908
  290.2 10.5 %collective-permute-start.29 = (bf16[48,2432]{1,0:T(8,128)(2,1)S(1)}, bf16[48,2432]{1,0:T(8,128)(2,1)S(1)}, u32[]{:S(2)}, u32[]{:S(2)}) collective-permute-start(bf16[48,2432]{1,0:T(8,128)(2,1)S(1)} %add_convert_fusion.11), channel_id=1, source_target_pairs={{0,16},{8,24},{16,0},{24,8},{1,17},{9,25},{17,1},{25,9},{2,18},{10... | collective-permute-start | bytes 700424 | tf_op jit(solution)/shard_map/ppermute | solution.py:908
  301.6 5.2 %collective-permute-start.28 = (bf16[96,768]{1,0:T(8,128)(2,1)S(1)}, bf16[96,768]{1,0:T(8,128)(2,1)S(1)}, u32[]{:S(2)}, u32[]{:S(2)}) collective-permute-start(bf16[96,768]{1,0:T(8,128)(2,1)S(1)} %add_convert_fusion.12), channel_id=1, source_target_pairs={{0,8},{8,0},{16,24},{24,16},{1,9},{9,1},{17,25},{25,17},{2,10},{10... | collective-permute-start | bytes 442376 | tf_op jit(solution)/shard_map/ppermute | solution.py:908
  307.8 11.4 %collective-permute-start.30 = (bf16[48,768]{1,0:T(8,128)(2,1)S(1)}, bf16[48,768]{1,0:T(8,128)(2,1)S(1)}, u32[]{:S(2)}, u32[]{:S(2)}) collective-permute-start(bf16[48,768]{1,0:T(8,128)(2,1)S(1)} %add_convert_fusion.14), channel_id=1, source_target_pairs={{0,16},{8,24},{16,0},{24,8},{1,17},{9,25},{17,1},{25,9},{2,18},{10... | collective-permute-start | bytes 221192 | tf_op jit(solution)/shard_map/ppermute | solution.py:908
  320.2 13.5 %collective-permute-start.31 = (bf16[48,1664]{1,0:T(8,128)(2,1)S(1)}, bf16[48,1664]{1,0:T(8,128)(2,1)S(1)}, u32[]{:S(2)}, u32[]{:S(2)}) collective-permute-start(bf16[48,1664]{1,0:T(8,128)(2,1)S(1)} %pad_maximum_fusion.5), channel_id=1, source_target_pairs={{0,16},{8,24},{16,0},{24,8},{1,17},{9,25},{17,1},{25,9},{2,18},{10... | collective-permute-start | bytes 479240 | tf_op jit(solution)/shard_map/ppermute | solution.py:908
  333.7 7.4 %collective-permute-start.32 = (bf16[96,1664]{1,0:T(8,128)(2,1)S(1)}, bf16[96,1664]{1,0:T(8,128)(2,1)S(1)}, u32[]{:S(2)}, u32[]{:S(2)}) collective-permute-start(bf16[96,1664]{1,0:T(8,128)(2,1)S(1)} %pad_maximum_fusion.4), channel_id=1, source_target_pairs={{0,8},{8,0},{16,24},{24,16},{1,9},{9,1},{17,25},{25,17},{2,10},{10... | collective-permute-start | bytes 958472 | tf_op jit(solution)/shard_map/ppermute | solution.py:908
  341.2 33.6 %collective-permute-start.33 = (bf16[192,1664]{1,0:T(8,128)(2,1)S(1)}, bf16[192,1664]{1,0:T(8,128)(2,1)S(1)}, u32[]{:S(2)}, u32[]{:S(2)}) collective-permute-start(bf16[192,1664]{1,0:T(8,128)(2,1)S(1)} %pad_maximum_fusion.1), channel_id=1, source_target_pairs={{0,4},{4,0},{1,5},{5,1},{2,6},{6,2},{3,7},{7,3},{8,12},{12,8},{9,1... | collective-permute-start | bytes 1916936 | tf_op jit(solution)/shard_map/ppermute | solution.py:908
  (43 other events, 343.1 us)
Sparse Core Ops, SparseCore 0:
  10.9 64.5 all-gather.5
  158.9 52.6 all-gather.7
  213.9 38.1 reduce-scatter.1
  301.7 86.1 all-gather.9
